TPU v7x, 32 devices: a whole 2x2x4 slice. The times are simulated.
32 devices in a mesh: ra: 4 (over z), dec: 8 (over y, x, core).
Axes of the slice: x: 2, y: 2, z: 4, core: 2. Of those that a mesh axis runs over, the one named last changes fastest.
Arguments:
- forests: bfloat16 [8, 32, 128, 1024], P('ra', 'dec'), may hold values from -6 to 6
- resolution: float32 [8, 32, 128], P('ra', 'dec'), may hold values from 0.3 to 1.2
- pixel_range: int32 [8, 32, 2, 128], P('ra', 'dec'), may hold values from 0 to 1024, as said below
- block_pairs: int32 [4, 8, 40, 3], P('ra', 'dec'), may hold values from -1 to 7, as said below
- block_count: int32 [4, 8], P('ra', 'dec'), may hold values from 10 to 40, as said below
- separation_bin: int32 [4, 8, 40, 128, 128], P('ra', 'dec'), may hold values from 0 to 8
Outputs:
- tile_power: float32 [4, 8, 8, 128], P('ra', 'dec')
- sky_power: float32 [8, 128], replicated
Inputs may be any that keep to these rules, and one draw needn't show every extreme that they name: `pixel_range`: lo < hi for every forest; at least 256 valid pixels. `block_pairs`: each device's list names every one of its own cells once with each of the five offsets (0, 0), (0, 1), (1, -1), (1, 0), (1, 1), in an order drawn from the seed. Slots at or past block_count are ignored. `block_count`: some device has all 40 slots live in every draw.
All inputs are finite; a program needn't handle non-finite values.
Results may differ from a plain program's by a relative error of at most 0.0037.
Values may be sent and summed in bfloat16 or wider, within the bound.
No kernel may reach another device: no remote copies, remote signals or barrier semaphores. Data moves between devices by JAX's collectives and lax.ppermute only.
A program may use at most 64 MiB of HBM per device.

v0:
```python
import jax
import jax.numpy as jnp
import numpy as np
from jax import lax
from jax.experimental import pallas as pl
from jax.experimental.pallas import tpu as pltpu
from jax.sharding import PartitionSpec as P

NSEP = 8
NKB = 128
VMEM_LIMIT = 32 * 2**20
OFFSETS = ((0, 0), (0, 1), (1, -1), (1, 0), (1, 1))

SINE_TILE = 2


def dft_table(length, n_bins):
    per_bin = length // 2 // n_bins
    sample = np.arange(length // 2)[:, None]
    blocks = []
    for q in range(0, per_bin, 2):
        modes = [np.arange(n_bins)[None, :] * per_bin + q + s for s in (0, 1)]
        angles = [2.0 * np.pi * (sample * mode % length) / length for mode in modes]
        tiles = [np.cos(angle) for angle in angles] + [np.sin(angle) for angle in angles]
        blocks.append(np.concatenate(tiles, axis=1))
    return np.stack(blocks).astype(np.float32).astype(jnp.bfloat16)


def pair_up(edges):
    at = {}
    for edge in edges:
        for cell in {edge[1], edge[2]}:
            at.setdefault(cell, []).append(edge)
    seen, used, groups, rest = set(), set(), [], []

    def visit(cell, up):
        seen.add(cell)
        pending = []
        for edge in at[cell]:
            if edge in used or edge is up:
                continue
            other = edge[2] if edge[1] == cell else edge[1]
            used.add(edge)
            if other == cell or other in seen or not visit(other, edge):
                pending.append(edge)
        pending.sort(key=lambda edge: edge[3])
        taken = len(pending) % 2 == 1 and up is not None
        if taken:
            pending.append(up)
        elif len(pending) % 2:
            rest.append(pending.pop())
        for i in range(0, len(pending), 2):
            groups.append((cell, pending[i : i + 2]))
        return taken

    for cell in sorted(at, reverse=True):
        if cell not in seen:
            visit(cell, None)
    return groups, rest


def plan(rows, cols):
    def arrival(cell):
        r, c = cell
        if r == rows:
            return 1 if c in (0, cols - 1) else 2
        return 0 if c < cols else 1

    edges, handed = [], []
    for r in range(rows):
        for c in range(cols):
            for d, (up, side) in enumerate(OFFSETS):
                a, b = (r, c), (r + up, c + side)
                key = (r * cols + c) * len(OFFSETS) + d
                if b[1] < 0:
                    handed.append(key)
                else:
                    edges.append((key, a, b, max(arrival(a), arrival(b))))
    stages = [[], [], []]
    groups, rest = pair_up([edge for edge in edges if edge[3] < 2])
    for group in groups:
        stages[max(edge[3] for edge in group[1])].append(group)
    groups, rest = pair_up(rest + [edge for edge in edges if edge[3] == 2])
    stages[2] = groups + [(edge[1], [edge]) for edge in rest]
    return stages, handed


def binned(sums, first):
    return (sums[0] + jnp.where(first, 0.0, sums[1])).sum(axis=1)


class Spectra:
    def __init__(self, cells, forests, basis, ranges, widths, scratch):
        (self.flux, self.table, self.masked, self.ranges, self.widths, sems, more_sems) = scratch
        self.cells = cells
        self.flux_copies = [
            pltpu.make_async_copy(forests.at[r, c], self.flux.at[i], sems.at[i])
            for i, (r, c) in enumerate(cells)
        ]
        self.form_copies = [
            pltpu.make_async_copy(ranges, self.ranges, more_sems.at[0]),
            pltpu.make_async_copy(widths, self.widths, more_sems.at[1]),
        ]
        self.table_copies = [
            pltpu.make_async_copy(basis.at[i], self.table.at[i], more_sems.at[2 + i])
            for i in range(basis.shape[0])
        ]

    def start(self):
        for copy in self.form_copies + self.flux_copies + self.table_copies:
            copy.start()

    def mask(self):
        count, per_cell, length = self.flux.shape
        for copy in self.form_copies:
            copy.wait()
        rows = []
        for r, c in self.cells:
            rows += [self.ranges[r, c].astype(jnp.float32), self.widths[r, c : c + 1]]
        filler = -3 * count % 8
        if filler:
            rows.append(jnp.zeros((filler, per_cell), jnp.float32))
        columns = jnp.concatenate(rows, axis=0).T
        step = 16
        position = lax.broadcasted_iota(jnp.int32, (step, length), 1).astype(jnp.float32)
        self.width = []
        for i in range(count):
            low, high, width = (columns[:, 3 * i + j : 3 * i + j + 1] for j in range(3))
            self.width.append(width)
            self.flux_copies[i].wait()
            for row in range(0, per_cell, step):
                inside = (position >= low[row : row + step]) & (position < high[row : row + step])
                kept = jnp.where(inside, self.flux[i, row : row + step].astype(jnp.float32), 0.0)
                start = i * per_cell + row
                self.masked[start : start + step] = kept.astype(jnp.bfloat16)

    def half(self, index, stores):
        _, per_cell, length = self.flux.shape
        per_bin = length // 2 // NKB
        lane = lax.broadcasted_iota(jnp.int32, (1, NKB), 1) * per_bin
        waves = [
            (lane + q).astype(jnp.float32) * (2.0 * jnp.pi / length)
            for q in (2 * index, 2 * index + 1)
        ]
        table = self.table[index]
        tiles = [table[:, i * NKB : (i + 1) * NKB] for i in range(4)]
        later = jnp.concatenate([tiles[0], -tiles[1], tiles[2], -tiles[3]], axis=1)
        raw = jnp.dot(
            self.masked[...],
            jnp.concatenate([table, later], axis=0),
            preferred_element_type=jnp.float32,
        )
        for i in range(len(self.cells)):
            windows = [jnp.exp(-0.5 * (wave * self.width[i]) ** 2) for wave in waves]
            for tile in range(4):
                part = raw[i * per_cell : (i + 1) * per_cell, tile * NKB : (tile + 1) * NKB]
                value = (part * windows[tile % 2]).astype(jnp.bfloat16)
                start = (4 * index + tile) * NKB
                for ref, row in stores[i]:
                    ref[row : row + per_cell, start : start + NKB] = value


def spectra_scratch(count, per_cell, basis, ranges, widths):
    halves, _, _ = basis.shape
    length = 2 * basis.shape[1]
    return [
        pltpu.VMEM((count, per_cell, length), jnp.bfloat16),
        pltpu.VMEM(basis.shape, jnp.bfloat16),
        pltpu.VMEM((count * per_cell, length), jnp.bfloat16),
        pltpu.VMEM(ranges.shape, jnp.int32),
        pltpu.VMEM(widths.shape, jnp.float32),
        pltpu.SemaphoreType.DMA((count,)),
        pltpu.SemaphoreType.DMA((2 + halves,)),
    ]


def vmem(n):
    return [pl.BlockSpec(memory_space=pltpu.VMEM)] * n


def in_hbm(value):
    return pltpu.with_memory_space_constraint(value, pltpu.HBM)


def params():
    return pltpu.CompilerParams(vmem_limit_bytes=VMEM_LIMIT)


def cost(flops, nbytes):
    return pl.CostEstimate(flops=int(flops), bytes_accessed=int(nbytes), transcendentals=0)


def first_row(forests, ranges, widths, basis):
    _, cols, per_cell, length = forests.shape

    def kernel(forests, ranges, widths, basis, ends, middle, *scratch):
        cells = [(0, c) for c in range(cols)]
        spectra = Spectra(cells, forests, basis, ranges, widths, scratch)
        spectra.start()
        spectra.mask()
        stores = [[(ends, 0)]] + [[(middle, i * per_cell)] for i in range(cols - 2)]
        stores.append([(ends, per_cell)])
        for index in range(basis.shape[0]):
            spectra.table_copies[index].wait()
            spectra.half(index, stores)

    return pl.pallas_call(
        kernel,
        name="first_row",
        out_shape=[
            jax.ShapeDtypeStruct((n * per_cell, length), jnp.bfloat16) for n in (2, cols - 2)
        ],
        in_specs=[pl.BlockSpec(memory_space=pltpu.HBM)] * 4,
        out_specs=vmem(2),
        scratch_shapes=spectra_scratch(cols, per_cell, basis, ranges, widths),
        compiler_params=params(),
        cost_estimate=cost(2 * cols * per_cell * length * length, 5 * 2**20),
    )(in_hbm(forests), in_hbm(ranges), in_hbm(widths), in_hbm(basis))


def other_rows(forests, ranges, widths, basis, ends, entries, bins, stages, handed):
    rows, cols, per_cell, length = forests.shape
    slots = bins.shape[0]
    cells = [(r, c) for r in range(1, rows) for c in range(cols)]
    sizes = [sum(len(group[1]) for group in stage) for stage in stages]
    strip = per_cell * per_cell // length
    n_basis = basis.shape[0]

    def kernel(*refs):
        forests, ranges, widths, basis, ends, entries, bins = refs[:7]
        own, low, counts = refs[7:10]
        sorted_bins, scratch = refs[10 : 10 + len(stages)], refs[10 + len(stages) :]
        entries_here, slot_of, list_sem = scratch[-3:]
        list_copy = pltpu.make_async_copy(entries, entries_here, list_sem)
        list_copy.start()
        spectra = Spectra(cells, forests, basis, ranges, widths, scratch[:-3])
        spectra.start()
        list_copy.wait()

        @pl.loop(0, slots)
        def _(s):
            cell, up, side, live = (entries_here[0, i, 0, s] for i in range(4))
            slot_of[cell * len(OFFSETS) + 3 * up + side] = jnp.where(s < live, s, s + slots)

        def bins_of(key):
            at = slot_of[key]
            dead = at >= slots
            block = bins[jnp.where(dead, at - slots, at)].astype(jnp.float32)
            return block + jnp.where(dead, float(NSEP), 0.0)

        spectra.mask()
        low[:per_cell] = ends[:per_cell]
        stores = []
        for i, (r, c) in enumerate(cells):
            stores.append([(own, i * per_cell)])
            if c == 0:
                stores[-1].append((low, r * per_cell))
        for index in range(n_basis):
            spectra.table_copies[index].wait()
            spectra.half(index, stores)
        for target, stage in zip(sorted_bins, stages):
            for i, (center, edge) in enumerate((c, edge) for c, pair in stage for edge in pair):
                block = bins_of(edge[0])
                target[i] = (block if center == edge[1] else block.T).astype(jnp.bfloat16)
        found = [jnp.zeros((8, per_cell), jnp.float32) for _ in range(NSEP)]
        for r, key in enumerate(handed):
            block = bins_of(key)
            for t in range(NSEP):
                one = jnp.where(block == float(t), 1.0, 0.0)
                found[t] = found[t] + one.reshape(per_cell // 8, 8, per_cell).sum(axis=0)
            block = block.astype(jnp.bfloat16)
            start = rows * per_cell + r * strip
            for i in range(per_cell // strip):
                low[start : start + strip, i * per_cell : (i + 1) * per_cell] = (
                    block[i * strip : (i + 1) * strip]
                )
        for t in range(NSEP):
            counts[t] = found[t]

    hbm, anywhere = (pl.BlockSpec(memory_space=space) for space in (pltpu.HBM, pl.ANY))
    bf16, f32 = jnp.bfloat16, jnp.float32
    shapes = [((rows - 1) * cols * per_cell, length), (rows * (per_cell + strip), length)]
    shapes = [jax.ShapeDtypeStruct(shape, bf16) for shape in shapes]
    shapes.append(jax.ShapeDtypeStruct((NSEP, 8, per_cell), f32))
    shapes += [jax.ShapeDtypeStruct((size, per_cell, per_cell), bf16) for size in sizes]
    return pl.pallas_call(
        kernel,
        name="other_rows",
        out_shape=shapes,
        in_specs=[hbm] * 4 + vmem(1) + [anywhere] + vmem(1),
        out_specs=vmem(len(shapes)),
        scratch_shapes=spectra_scratch(len(cells), per_cell, basis, ranges, widths)
        + [
            pltpu.SMEM(entries.shape, jnp.int32),
            pltpu.SMEM((slots,), jnp.int32),
            pltpu.SemaphoreType.DMA,
        ],
        compiler_params=params(),
        cost_estimate=cost(2 * len(cells) * per_cell * length * length, 8 * 2**20),
    )(
        in_hbm(forests),
        in_hbm(ranges),
        in_hbm(widths),
        in_hbm(basis),
        ends,
        entries,
        bins,
    )


def pair_sums(groups, given, bins, arrays, place, carried, per_cell, last):
    length = arrays[0].shape[1]
    n_arrays, n_carried = len(arrays), len(carried)
    span = 2 * NKB
    strip = per_cell * per_cell // length

    def kernel(*refs):
        arrays, bins = refs[:n_arrays], refs[n_arrays]
        carried = refs[n_arrays + 1 : n_arrays + 1 + n_carried]
        outs, chosen = refs[n_arrays + 1 + n_carried : -1], refs[-1]
        lane = lax.broadcasted_iota(jnp.int32, (per_cell, NKB), 1)
        unit = jnp.where(lane == 0, 1.0, 0.0).astype(jnp.bfloat16)
        first = lax.broadcasted_iota(jnp.int32, (NSEP, 8, NKB), 2) == 0

        def columns(cell, n):
            array, row = place[cell]
            value = arrays[array][row : row + per_cell, n * span : (n + 1) * span]
            if n != SINE_TILE // 2:
                return value
            return jnp.concatenate([value[:, :NKB] + unit, value[:, NKB:]], axis=1)

        def choose(e, block, row, column):
            for t in range(NSEP):
                start = t * per_cell + row
                e[start : start + block.shape[0], column : column + per_cell] = jnp.where(
                    block == jnp.bfloat16(t), jnp.bfloat16(1), jnp.bfloat16(0)
                )

        def add(sums, e, center, others):
            onehot = e[:, : len(others) * per_cell]
            for n in range(length // span):
                right = jnp.concatenate([columns(other, n) for other in others], axis=0)
                mixed = jnp.dot(onehot, right, preferred_element_type=jnp.float32)
                left = columns(center, n).astype(jnp.float32)
                term = mixed.reshape(NSEP, per_cell, span) * left[None]
                term = term.reshape(NSEP, per_cell // 8, 8, span).sum(axis=1)
                for s in (0, 1):
                    which = int(2 * n + s == SINE_TILE)
                    sums[which] = sums[which] + term[:, :, s * NKB : (s + 1) * NKB]

        def zeros():
            return [jnp.zeros((NSEP, 8, NKB), jnp.float32) for _ in range(2)]

        sums, others_sums = zeros(), zeros()
        position = turn = 0
        for center, pair in groups:
            e = chosen.at[turn % 2]
            turn += 1
            for o in range(len(pair)):
                choose(e, bins[position + o], 0, o * per_cell)
            position += len(pair)
            add(sums, e, center, [edge[1] if center != edge[1] else edge[2] for edge in pair])
        for array, start, a, b in given:
            e = chosen.at[turn % 2]
            turn += 1
            for i in range(per_cell // strip):
                piece = arrays[array][start : start + strip, i * per_cell : (i + 1) * per_cell]
                choose(e, piece, i * strip, 0)
            add(others_sums, e, a, [b])
        if not last:
            for which in (0, 1):
                outs[0][which] = sums[which]
            if given:
                outs[1][...] = binned(others_sums, first)
            return
        *partials, left_out, for_others = carried
        for partial in partials:
            sums = [sums[which] + partial[which] for which in (0, 1)]
        own = binned(sums, first)
        outs[0][...] = own
        outs[1][:NSEP] = own + for_others[...]
        counts = (jnp.where(first, sums[1], 0.0) + left_out[...]).sum(axis=1)
        outs[1][NSEP:] = jnp.broadcast_to(counts.sum(axis=1, keepdims=True), (NSEP, NKB))

    if last:
        shapes = [(NSEP, NKB), (2 * NSEP, NKB)]
    else:
        shapes = [(2, NSEP, 8, NKB)] + [(NSEP, NKB)] * bool(given)
    n_edges = sum(len(group[1]) for group in groups) + len(given)
    return pl.pallas_call(
        kernel,
        out_shape=[jax.ShapeDtypeStruct(shape, jnp.float32) for shape in shapes],
        in_specs=vmem(n_arrays + 1 + n_carried),
        out_specs=vmem(len(shapes)),
        scratch_shapes=[pltpu.VMEM((2, NSEP * per_cell, 2 * per_cell), jnp.bfloat16)],
        compiler_params=params(),
        cost_estimate=cost(2 * NSEP * per_cell * per_cell * length * n_edges, 2**20),
    )(*arrays, bins, *carried)


def over_mesh(value, axes):
    for axis in axes:
        count = lax.axis_size(axis)
        if count & (count - 1):
            value = lax.psum(value, axis)
            continue
        step = 1
        while step < count:
            value = value + lax.ppermute(value, axis, [(i, i ^ step) for i in range(count)])
            step *= 2
    return value


def shifted(value, axis, steps):
    count = lax.axis_size(axis)
    return lax.ppermute(
        value, axis, [(i + steps, i) for i in range(count) if 0 <= i + steps < count]
    )


def per_device(forests, resolution, pixel_range, block_pairs, block_count, separation_bin):
    rows, cols, per_cell, length = forests.shape
    stages, handed = plan(rows, cols)
    table = dft_table(length, NKB)
    basis = jnp.asarray(table)
    live = jnp.broadcast_to(block_count[..., None, None], (1, 1, 1, block_pairs.shape[2]))
    entries = jnp.concatenate([block_pairs.transpose(0, 3, 1, 2), live], axis=1)
    ends, middle = first_row(forests, pixel_range, resolution, basis)
    above_ends = shifted(ends, "ra", 1)
    above_middle = shifted(middle, "ra", 1)
    own, low, counts, *bins = other_rows(
        forests,
        pixel_range,
        resolution,
        basis,
        ends,
        entries,
        separation_bin[0, 0],
        stages,
        handed,
    )
    right = shifted(low, "dec", 1)

    place = {(0, 0): (0, 0), (0, cols - 1): (0, 1)}
    place |= {(0, c): (1, c - 1) for c in range(1, cols - 1)}
    place |= {(r, c): (2, (r - 1) * cols + c) for r in range(1, rows) for c in range(cols)}
    place |= {(r, cols): (3, r) for r in range(rows)}
    place |= {(rows, 0): (4, 0), (rows, cols - 1): (4, 1)}
    place |= {(rows, c): (5, c - 1) for c in range(1, cols - 1)}
    place |= {(rows, cols): (6, 0)}
    strip = per_cell * per_cell // length
    given = [(3, rows * per_cell + r * strip, (r, cols), (r + 1, cols - 1)) for r in range(rows)]

    def sums(stage, arrays, given, carried):
        cells = {cell for _, pair in stages[stage] for edge in pair for cell in edge[1:3]}
        cells |= {cell for one in given for cell in one[2:]}
        named = sorted({place[cell][0] for cell in cells})
        local = {cell: (named.index(place[cell][0]), place[cell][1] * per_cell) for cell in cells}
        return pair_sums(
            stages[stage],
            [(named.index(one[0]), *one[1:]) for one in given],
            bins[stage],
            [arrays[i] for i in named],
            local,
            carried,
            per_cell,
            stage == len(stages) - 1,
        )

    arrays = [ends, middle, own, right, above_ends, above_middle]
    (partial,) = sums(0, arrays, [], [])
    above_ends, partial = lax.optimization_barrier((above_ends, partial))
    arrays[4] = above_ends
    arrays.append(shifted(above_ends[:per_cell], "dec", 1))
    partial_too, for_others = sums(1, arrays, given, [])
    from_left = shifted(for_others, "dec", -1)
    own_sums, result = sums(2, arrays, [], [partial, partial_too, counts, for_others])
    tile_power = ((own_sums + from_left) / (per_cell * length)).reshape(1, 1, NSEP, NKB)
    total = over_mesh(result, ("dec", "ra"))
    sky_power = total[:NSEP] / jnp.maximum(total[NSEP:], 1.0)
    return tile_power, sky_power


def solution(mesh):
    in_specs = (
        P("ra", "dec", None, None),
        P("ra", "dec", None),
        P("ra", "dec", None, None),
        P("ra", "dec", None, None),
        P("ra", "dec"),
        P("ra", "dec", None, None, None),
    )
    out_specs = (P("ra", "dec", None, None), P())
    return jax.shard_map(
        per_device, mesh=mesh, in_specs=in_specs, out_specs=out_specs, check_vma=False
    )
```

profile of v0, /device:TPU:0, one launch (start us, length us, event | category | flops | bytes accessed | tf_op | source)
XLA Modules:
  0.0 59.2 jit_solution(2869437720346059504)
XLA Ops:
  0.6 0.0 copy-start
  1.4 0.7 %concatenate.3.refs_5_ = s32[1,4,1,40]{3,2,1,0:T(1,128)S(1)} pad(s32[1,3,1,40]{3,2,1,0:T(1,128)} %bitcast.7, s32[]{:T(128)} %bitcast.5), padding=0_0x0_1x0_0x0_0 | pad | bytes 1124 | tf_op jit(solution)/shard_map/concatenate | solution.py:427
  2.1 3.0 %first_row.1 = (bf16[256,1024]{1,0:T(8,128)(2,1)S(1)}, bf16[256,1024]{1,0:T(8,128)(2,1)S(1)}) custom-call(bf16[2,4,128,1024]{3,2,1,0:T(8,128)(2,1)} %refs_0_.1, s32[2,4,2,128]{3,2,1,0:T(2,128)} %refs_1_.1, f32[2,4,128]{2,1,0:T(4,128)} %refs_2_.1, bf16[2,512,512]{2,1,0:T(8,128)(2,1)} %constant.7.clone.basis.refs_3_), custom_call_target="tpu_custom_call" | custom-call | flops 1073741824 | bytes 5242880 | tf_op jit(solution)/shard_map/first_row/pallas_call | solution.py:207
  5.1 0.0 copy-done
  5.1 3.5 %other_rows.1 = (bf16[512,1024]{1,0:T(8,128)(2,1)S(1)}, bf16[288,1024]{1,0:T(8,128)(2,1)S(1)}, f32[8,8,128]{2,1,0:T(8,128)S(1)}, bf16[22,128,128]{2,1,0:T(8,128)...) custom-call(bf16[2,4,128,1024]{3,2,1,0:T(8,128)(2,1)} %refs_0_.1, ...), custom_call_target="tpu_custom_call" | custom-call | flops 1073741824 | bytes 8388608 | tf_op jit(solution)/shard_map/other_rows/pallas_call | solution.py:286
  8.6 1.3 %collective-permute-start.3 = (bf16[288,1024]{1,0:T(8,128)(2,1)S(1)}, bf16[288,1024]{1,0:T(8,128)(2,1)S(1)}, u32[]{:S(2)}, u32[]{:S(2)}) collective-permute-start(bf16[288,1024]{1,0:T(8,128)(2,1)S(1)} %get-tuple-element.23), channel_id=1, source_target_pairs={{1,0},{2,1},{3,2},{4,3},{5,4},{6,5},{7,6},{9,8},{10,9},{11,10},{12... | collective-permute-start | bytes 1769480 | tf_op jit(solution)/shard_map/ppermute | solution.py:416
  9.9 1.3 %collective-permute-start = (bf16[256,1024]{1,0:T(8,128)(2,1)S(1)}, bf16[256,1024]{1,0:T(8,128)(2,1)S(1)}, u32[]{:S(2)}, u32[]{:S(2)}) collective-permute-start(bf16[256,1024]{1,0:T(8,128)(2,1)S(1)} %get-tuple-element.16.refs_4_.refs_0_), channel_id=1, source_target_pairs={{8,0},{16,8},{24,16},{9,1},{17,9},{25,17},{10,2},{18,10},{26,18},{... | collective-permute-start | bytes 1572872 | tf_op jit(solution)/shard_map/ppermute | solution.py:416
  11.2 1.3 %collective-permute-start.1 = (bf16[256,1024]{1,0:T(8,128)(2,1)S(1)}, bf16[256,1024]{1,0:T(8,128)(2,1)S(1)}, u32[]{:S(2)}, u32[]{:S(2)}) collective-permute-start(bf16[256,1024]{1,0:T(8,128)(2,1)S(1)} %get-tuple-element.18.refs_1_), channel_id=1, source_target_pairs={{8,0},{16,8},{24,16},{9,1},{17,9},{25,17},{10,2},{18,10},{26,18},{... | collective-permute-start | bytes 1572872 | tf_op jit(solution)/shard_map/ppermute | solution.py:416
  12.5 6.9 %shard_map.86.refs_5_ = f32[2,8,8,128]{3,2,1,0:T(8,128)S(1)} custom-call(bf16[256,1024]{1,0:T(8,128)(2,1)S(1)} %get-tuple-element.16.refs_4_.refs_0_, bf16[256,1024]{1,0:T(8,128)(2,1)S(1)} %get-tuple-element.18.refs_1_, bf16[512,1024]{1,0:T(8,128)(2,1)S(1)} %get-tuple-element.17.refs_2_.refs_1_.refs_0_, bf16[22,128,128]{2,1,0:T(8,128)(2,1)S(1)} %get-tuple-element.19.refs_3_), custom_call_target="tpu_custom_call" | custom-call | flops 5905580032 | bytes 1048576 | tf_op jit(solution)/shard_map/pallas_call | solution.py:390
  19.4 7.8 %collective-permute-done.refs_3_.refs_1_ = bf16[256,1024]{1,0:T(8,128)(2,1)S(1)} collective-permute-done((bf16[256,1024]{1,0:T(8,128)(2,1)S(1)}, bf16[256,1024]{1,0:T(8,128)(2,1)S(1)}, u32[]{:S(2)}, u32[]{:S(2)}) %collective-permute-start) | collective-permute-done | bytes 524320 | tf_op jit(solution)/shard_map/ppermute | solution.py:416
  27.2 1.5 %collective-permute-start.2 = (bf16[128,1024]{1,0:T(8,128)(2,1)S(1)}, bf16[128,1024]{1,0:T(8,128)(2,1)S(1)}, u32[]{:S(2)}, u32[]{:S(2)}) collective-permute-start(bf16[128,1024]{1,0:T(8,128)(2,1)S(1)} %slice.9), channel_id=1, source_target_pairs={{1,0},{2,1},{3,2},{4,3},{5,4},{6,5},{7,6},{9,8},{10,9},{11,10},{12... | collective-permute-start | bytes 786440 | tf_op jit(solution)/shard_map/ppermute | solution.py:416
  28.7 0.0 collective-permute-done.3.refs_2_
  28.7 4.0 %shard_map.87 = (f32[2,8,8,128]{3,2,1,0:T(8,128)S(1)}, f32[8,128]{1,0:T(8,128)S(1)}) custom-call(bf16[256,1024]{1,0:T(8,128)(2,1)S(1)} %get-tuple-element.16.refs_4_.refs_0_, bf16[512,1024]{1,0:T(8,128)(2,1)S(1)} %get-tuple-element.17.refs_2_.refs_1_.refs_0_, bf16[288,1024]{1,0:T(8,128)(2,1)S(1)} %collective-permute-done.3.refs_2_, ...), custom_call_target="tpu_custom_call" | custom-call | flops 2684354560 | bytes 1048576 | tf_op jit(solution)/shard_map/pallas_call | solution.py:390
  32.7 5.7 %collective-permute-done.1.refs_2_ = bf16[256,1024]{1,0:T(8,128)(2,1)S(1)} collective-permute-done((bf16[256,1024]{1,0:T(8,128)(2,1)S(1)}, bf16[256,1024]{1,0:T(8,128)(2,1)S(1)}, u32[]{:S(2)}, u32[]{:S(2)}) %collective-permute-start.1) | collective-permute-done | bytes 524320 | tf_op jit(solution)/shard_map/ppermute | solution.py:416
  38.4 0.0 collective-permute-done.2.refs_3_
  38.5 2.8 %shard_map.88 = (f32[8,128]{1,0:T(8,128)S(1)}, f32[16,128]{1,0:T(8,128)S(1)}) custom-call(bf16[512,1024]{1,0:T(8,128)(2,1)S(1)} %get-tuple-element.17.refs_2_.refs_1_.refs_0_, bf16[256,1024]{1,0:T(8,128)(2,1)S(1)} %collective-permute-done.refs_3_.refs_1_, bf16[256,1024]{1,0:T(8,128)(2,1)S(1)} %collective-permute-done.1.refs_2_, ...), custom_call_target="tpu_custom_call" | custom-call | flops 2147483648 | bytes 1048576 | tf_op jit(solution)/shard_map/pallas_call | solution.py:390
  41.3 0.3 collective-permute-start.5
  41.6 0.9 %collective-permute-done.5 = f32[16,128]{1,0:T(8,128)S(1)} collective-permute-done((f32[16,128]{1,0:T(8,128)S(1)}, f32[16,128]{1,0:T(8,128)S(1)}, u32[]{:S(2)}, u32[]{:S(2)}) %collective-permute-start.5) | collective-permute-done | bytes 8224 | tf_op jit(solution)/shard_map/ppermute | solution.py:409
  42.5 2.5 %collective-permute-start.6 = (f32[16,128]{1,0:T(8,128)S(1)}, f32[16,128]{1,0:T(8,128)S(1)}, u32[]{:S(2)}, u32[]{:S(2)}) collective-permute-start(f32[16,128]{1,0:T(8,128)S(1)} %add.21), channel_id=1, source_target_pairs={{0,2},{1,3},{2,0},{3,1},{4,6},{5,7},{6,4},{7,5},{8,10},{9,11},{10,... | collective-permute-start | bytes 24584 | tf_op jit(solution)/shard_map/ppermute | solution.py:409
  45.0 1.6 %collective-permute-done.6 = f32[16,128]{1,0:T(8,128)S(1)} collective-permute-done((f32[16,128]{1,0:T(8,128)S(1)}, f32[16,128]{1,0:T(8,128)S(1)}, u32[]{:S(2)}, u32[]{:S(2)}) %collective-permute-start.6) | collective-permute-done | bytes 8224 | tf_op jit(solution)/shard_map/ppermute | solution.py:409
  46.7 2.0 %collective-permute-start.7 = (f32[16,128]{1,0:T(8,128)S(1)}, f32[16,128]{1,0:T(8,128)S(1)}, u32[]{:S(2)}, u32[]{:S(2)}) collective-permute-start(f32[16,128]{1,0:T(8,128)S(1)} %add.22), channel_id=1, source_target_pairs={{0,4},{1,5},{2,6},{3,7},{4,0},{5,1},{6,2},{7,3},{8,12},{9,13},{10,... | collective-permute-start | bytes 24584 | tf_op jit(solution)/shard_map/ppermute | solution.py:409
  48.7 1.6 %collective-permute-done.7 = f32[16,128]{1,0:T(8,128)S(1)} collective-permute-done((f32[16,128]{1,0:T(8,128)S(1)}, f32[16,128]{1,0:T(8,128)S(1)}, u32[]{:S(2)}, u32[]{:S(2)}) %collective-permute-start.7) | collective-permute-done | bytes 8224 | tf_op jit(solution)/shard_map/ppermute | solution.py:409
  50.4 1.8 %collective-permute-start.8 = (f32[16,128]{1,0:T(8,128)S(1)}, f32[16,128]{1,0:T(8,128)S(1)}, u32[]{:S(2)}, u32[]{:S(2)}) collective-permute-start(f32[16,128]{1,0:T(8,128)S(1)} %add.23), channel_id=1, source_target_pairs={{0,8},{8,0},{16,24},{24,16},{1,9},{9,1},{17,25},{25,17},{2,10},{10... | collective-permute-start | bytes 24584 | tf_op jit(solution)/shard_map/ppermute | solution.py:409
  52.1 1.3 %collective-permute-start.4 = (f32[8,128]{1,0:T(8,128)S(1)}, f32[8,128]{1,0:T(8,128)S(1)}, u32[]{:S(2)}, u32[]{:S(2)}) collective-permute-start(f32[8,128]{1,0:T(8,128)S(1)} %get-tuple-element.27.refs_8_), channel_id=1, source_target_pairs={{0,1},{1,2},{2,3},{3,4},{4,5},{5,6},{6,7},{8,9},{9,10},{10,11},{11... | collective-permute-start | bytes 12296 | tf_op jit(solution)/shard_map/ppermute | solution.py:416
  53.4 0.6 %collective-permute-done.8 = f32[16,128]{1,0:T(8,128)S(1)} collective-permute-done((f32[16,128]{1,0:T(8,128)S(1)}, f32[16,128]{1,0:T(8,128)S(1)}, u32[]{:S(2)}, u32[]{:S(2)}) %collective-permute-start.8) | collective-permute-done | bytes 8224 | tf_op jit(solution)/shard_map/ppermute | solution.py:409
  54.0 2.8 %collective-permute-start.9 = (f32[16,128]{1,0:T(8,128)S(1)}, f32[16,128]{1,0:T(8,128)S(1)}, u32[]{:S(2)}, u32[]{:S(2)}) collective-permute-start(f32[16,128]{1,0:T(8,128)S(1)} %add.24), channel_id=1, source_target_pairs={{0,16},{8,24},{16,0},{24,8},{1,17},{9,25},{17,1},{25,9},{2,18},{10... | collective-permute-start | bytes 24584 | tf_op jit(solution)/shard_map/ppermute | solution.py:409
  56.8 0.0 collective-permute-done.4
  56.8 0.6 %multiply_bitcast_fusion = f32[1,1,8,128]{3,2,1,0:T(8,128)} fusion(f32[8,128]{1,0:T(8,128)S(1)} %get-tuple-element.28, f32[8,128]{1,0:T(8,128)S(1)} %collective-permute-done.4), kind=kLoop, calls=%fused_computation.2 | loop fusion | flops 2048 | bytes 12288 | tf_op jit(solution)/shard_map/reshape | solution.py:478
  57.4 1.2 %collective-permute-done.9 = f32[16,128]{1,0:T(8,128)S(1)} collective-permute-done((f32[16,128]{1,0:T(8,128)S(1)}, f32[16,128]{1,0:T(8,128)S(1)}, u32[]{:S(2)}, u32[]{:S(2)}) %collective-permute-start.9) | collective-permute-done | bytes 8224 | tf_op jit(solution)/shard_map/ppermute | solution.py:409
  58.6 0.6 %fusion = f32[8,128]{1,0:T(8,128)} fusion(f32[16,128]{1,0:T(8,128)S(1)} %add.25), kind=kLoop, calls=%fused_computation.1 | loop fusion | flops 2048 | bytes 12288 | tf_op jit(solution)/shard_map/div | solution.py:480
  (6 shorter events, 0.0 us)
Async XLA Ops:
  0.6 4.5 %copy-start = (s32[1,1,40,128,128]{4,3,2,1,0:T(8,128)S(1)}, s32[1,1,40,128,128]{4,3,2,1,0:T(8,128)}, u32[]{:S(2)}) copy-start(s32[1,1,40,128,128]{4,3,2,1,0:T(8,128)} %param.12) | copy-start | bytes 7864324
  8.6 20.1 %collective-permute-start.3 = (bf16[288,1024]{1,0:T(8,128)(2,1)S(1)}, bf16[288,1024]{1,0:T(8,128)(2,1)S(1)}, u32[]{:S(2)}, u32[]{:S(2)}) collective-permute-start(bf16[288,1024]{1,0:T(8,128)(2,1)S(1)} %get-tuple-element.23), channel_id=1, source_target_pairs={{1,0},{2,1},{3,2},{4,3},{5,4},{6,5},{7,6},{9,8},{10,9},{11,10},{12... | collective-permute-start | bytes 1769480 | tf_op jit(solution)/shard_map/ppermute | solution.py:416
  9.9 17.3 %collective-permute-start = (bf16[256,1024]{1,0:T(8,128)(2,1)S(1)}, bf16[256,1024]{1,0:T(8,128)(2,1)S(1)}, u32[]{:S(2)}, u32[]{:S(2)}) collective-permute-start(bf16[256,1024]{1,0:T(8,128)(2,1)S(1)} %get-tuple-element.16.refs_4_.refs_0_), channel_id=1, source_target_pairs={{8,0},{16,8},{24,16},{9,1},{17,9},{25,17},{10,2},{18,10},{26,18},{... | collective-permute-start | bytes 1572872 | tf_op jit(solution)/shard_map/ppermute | solution.py:416
  11.2 27.2 %collective-permute-start.1 = (bf16[256,1024]{1,0:T(8,128)(2,1)S(1)}, bf16[256,1024]{1,0:T(8,128)(2,1)S(1)}, u32[]{:S(2)}, u32[]{:S(2)}) collective-permute-start(bf16[256,1024]{1,0:T(8,128)(2,1)S(1)} %get-tuple-element.18.refs_1_), channel_id=1, source_target_pairs={{8,0},{16,8},{24,16},{9,1},{17,9},{25,17},{10,2},{18,10},{26,18},{... | collective-permute-start | bytes 1572872 | tf_op jit(solution)/shard_map/ppermute | solution.py:416
  27.2 11.2 %collective-permute-start.2 = (bf16[128,1024]{1,0:T(8,128)(2,1)S(1)}, bf16[128,1024]{1,0:T(8,128)(2,1)S(1)}, u32[]{:S(2)}, u32[]{:S(2)}) collective-permute-start(bf16[128,1024]{1,0:T(8,128)(2,1)S(1)} %slice.9), channel_id=1, source_target_pairs={{1,0},{2,1},{3,2},{4,3},{5,4},{6,5},{7,6},{9,8},{10,9},{11,10},{12... | collective-permute-start | bytes 786440 | tf_op jit(solution)/shard_map/ppermute | solution.py:416
  41.3 1.2 %collective-permute-start.5 = (f32[16,128]{1,0:T(8,128)S(1)}, f32[16,128]{1,0:T(8,128)S(1)}, u32[]{:S(2)}, u32[]{:S(2)}) collective-permute-start(f32[16,128]{1,0:T(8,128)S(1)} %get-tuple-element.29), channel_id=1, source_target_pairs={{0,1},{1,0},{2,3},{3,2},{4,5},{5,4},{6,7},{7,6},{8,9},{9,8},{10,11... | collective-permute-start | bytes 24584 | tf_op jit(solution)/shard_map/ppermute | solution.py:409
  42.5 4.2 %collective-permute-start.6 = (f32[16,128]{1,0:T(8,128)S(1)}, f32[16,128]{1,0:T(8,128)S(1)}, u32[]{:S(2)}, u32[]{:S(2)}) collective-permute-start(f32[16,128]{1,0:T(8,128)S(1)} %add.21), channel_id=1, source_target_pairs={{0,2},{1,3},{2,0},{3,1},{4,6},{5,7},{6,4},{7,5},{8,10},{9,11},{10,... | collective-permute-start | bytes 24584 | tf_op jit(solution)/shard_map/ppermute | solution.py:409
  46.7 3.7 %collective-permute-start.7 = (f32[16,128]{1,0:T(8,128)S(1)}, f32[16,128]{1,0:T(8,128)S(1)}, u32[]{:S(2)}, u32[]{:S(2)}) collective-permute-start(f32[16,128]{1,0:T(8,128)S(1)} %add.22), channel_id=1, source_target_pairs={{0,4},{1,5},{2,6},{3,7},{4,0},{5,1},{6,2},{7,3},{8,12},{9,13},{10,... | collective-permute-start | bytes 24584 | tf_op jit(solution)/shard_map/ppermute | solution.py:409
  50.4 3.7 %collective-permute-start.8 = (f32[16,128]{1,0:T(8,128)S(1)}, f32[16,128]{1,0:T(8,128)S(1)}, u32[]{:S(2)}, u32[]{:S(2)}) collective-permute-start(f32[16,128]{1,0:T(8,128)S(1)} %add.23), channel_id=1, source_target_pairs={{0,8},{8,0},{16,24},{24,16},{1,9},{9,1},{17,25},{25,17},{2,10},{10... | collective-permute-start | bytes 24584 | tf_op jit(solution)/shard_map/ppermute | solution.py:409
  52.1 4.7 %collective-permute-start.4 = (f32[8,128]{1,0:T(8,128)S(1)}, f32[8,128]{1,0:T(8,128)S(1)}, u32[]{:S(2)}, u32[]{:S(2)}) collective-permute-start(f32[8,128]{1,0:T(8,128)S(1)} %get-tuple-element.27.refs_8_), channel_id=1, source_target_pairs={{0,1},{1,2},{2,3},{3,4},{4,5},{5,6},{6,7},{8,9},{9,10},{10,11},{11... | collective-permute-start | bytes 12296 | tf_op jit(solution)/shard_map/ppermute | solution.py:416
  54.0 4.5 %collective-permute-start.9 = (f32[16,128]{1,0:T(8,128)S(1)}, f32[16,128]{1,0:T(8,128)S(1)}, u32[]{:S(2)}, u32[]{:S(2)}) collective-permute-start(f32[16,128]{1,0:T(8,128)S(1)} %add.24), channel_id=1, source_target_pairs={{0,16},{8,24},{16,0},{24,8},{1,17},{9,25},{17,1},{25,9},{2,18},{10... | collective-permute-start | bytes 24584 | tf_op jit(solution)/shard_map/ppermute | solution.py:409
where the time goes:
time: 59.9 us; the launch traced here: 59.2 us
  Pallas kernels  20.2 us (34%)
  waiting for transfers between devices  19.5 us (33%)
  starting transfers between devices  16.1 us (27%)
  between operations  1.53 us (3%)
  other arithmetic  1.22 us (2%)
  local copies, waits for them, and re-layouts  0.71 us (1%)
    pallas_call x3, Pallas kernels, pair_sums(): pl.pallas_call(kernel, out_shape=[jax.ShapeDtypeStruct(shape, jnp.float32...  13.7 us
    ppermute x5, waiting for transfers between devices, shifted(): lax.ppermute(value, axis, [(i + steps, i) for i in range(count) if 0 <= i...  13.5 us
    ppermute x5, starting transfers between devices, over_mesh(): lax.ppermute(value, axis, [(i, i ^ step) for i in range(count)])  9.44 us
    ppermute x5, starting transfers between devices, shifted(): lax.ppermute(value, axis, [(i + steps, i) for i in range(count) if 0 <= i...  6.63 us
    ppermute x5, waiting for transfers between devices, over_mesh(): lax.ppermute(value, axis, [(i, i ^ step) for i in range(count)])  5.93 us
    pallas_call x1, Pallas kernels, other_rows(): pl.pallas_call(kernel, name='other_rows', out_shape=shapes, in_specs=[hbm...  3.48 us
    pallas_call x1, Pallas kernels, first_row(): pl.pallas_call(kernel, name='first_row', out_shape=[jax.ShapeDtypeStruct(...  3 us
  transfers between devices with their start and end apart: 10, of which 7 were waited for; matrix products, arithmetic and copies ran while one was open for 1% of the time, Pallas kernels for 18%

commit v1 on v0

--- a/solution.py
+++ b/solution.py
@@ -190,46 +190,44 @@
     return pl.CostEstimate(flops=int(flops), bytes_accessed=int(nbytes), transcendentals=0)
 
 
-def first_row(forests, ranges, widths, basis):
+def end_cells(forests, ranges, widths, basis):
     _, cols, per_cell, length = forests.shape
-
-    def kernel(forests, ranges, widths, basis, ends, middle, *scratch):
-        cells = [(0, c) for c in range(cols)]
+    cells = [(0, 0), (0, cols - 1)]
+
+    def kernel(forests, ranges, widths, basis, ends, *scratch):
         spectra = Spectra(cells, forests, basis, ranges, widths, scratch)
         spectra.start()
         spectra.mask()
-        stores = [[(ends, 0)]] + [[(middle, i * per_cell)] for i in range(cols - 2)]
-        stores.append([(ends, per_cell)])
+        for copy in spectra.table_copies:
+            copy.wait()
         for index in range(basis.shape[0]):
-            spectra.table_copies[index].wait()
-            spectra.half(index, stores)
+            spectra.half(index, [[(ends, 0)], [(ends, per_cell)]])
 
     return pl.pallas_call(
         kernel,
-        name="first_row",
-        out_shape=[
-            jax.ShapeDtypeStruct((n * per_cell, length), jnp.bfloat16) for n in (2, cols - 2)
-        ],
+        name="end_cells",
+        out_shape=jax.ShapeDtypeStruct((2 * per_cell, length), jnp.bfloat16),
         in_specs=[pl.BlockSpec(memory_space=pltpu.HBM)] * 4,
-        out_specs=vmem(2),
-        scratch_shapes=spectra_scratch(cols, per_cell, basis, ranges, widths),
+        out_specs=pl.BlockSpec(memory_space=pltpu.VMEM),
+        scratch_shapes=spectra_scratch(2, per_cell, basis, ranges, widths),
         compiler_params=params(),
-        cost_estimate=cost(2 * cols * per_cell * length * length, 5 * 2**20),
+        cost_estimate=cost(4 * per_cell * length * length, 4 * 2**20),
     )(in_hbm(forests), in_hbm(ranges), in_hbm(widths), in_hbm(basis))
 
 
-def other_rows(forests, ranges, widths, basis, ends, entries, bins, stages, handed):
+def other_cells(forests, ranges, widths, basis, ends, entries, bins, stages, handed):
     rows, cols, per_cell, length = forests.shape
     slots = bins.shape[0]
-    cells = [(r, c) for r in range(1, rows) for c in range(cols)]
+    cells = [(0, c) for c in range(1, cols - 1)]
+    cells += [(r, c) for r in range(1, rows) for c in range(cols)]
     sizes = [sum(len(group[1]) for group in stage) for stage in stages]
     strip = per_cell * per_cell // length
     n_basis = basis.shape[0]
 
     def kernel(*refs):
         forests, ranges, widths, basis, ends, entries, bins = refs[:7]
-        own, low, counts = refs[7:10]
-        sorted_bins, scratch = refs[10 : 10 + len(stages)], refs[10 + len(stages) :]
+        middle, own, low, counts = refs[7:11]
+        sorted_bins, scratch = refs[11 : 11 + len(stages)], refs[11 + len(stages) :]
         entries_here, slot_of, list_sem = scratch[-3:]
         list_copy = pltpu.make_async_copy(entries, entries_here, list_sem)
         list_copy.start()
@@ -240,7 +238,7 @@
         @pl.loop(0, slots)
         def _(s):
             cell, up, side, live = (entries_here[0, i, 0, s] for i in range(4))
-            slot_of[cell * len(OFFSETS) + 3 * up + side] = jnp.where(s < live, s, s + slots)
+            slot_of[cell * len(OFFSETS) + 3 * up + side] = jnp.where(live > 0, s, s + slots)
 
         def bins_of(key):
             at = slot_of[key]
@@ -251,12 +249,16 @@
         spectra.mask()
         low[:per_cell] = ends[:per_cell]
         stores = []
-        for i, (r, c) in enumerate(cells):
-            stores.append([(own, i * per_cell)])
+        for r, c in cells:
+            if r == 0:
+                stores.append([(middle, (c - 1) * per_cell)])
+                continue
+            stores.append([(own, ((r - 1) * cols + c) * per_cell)])
             if c == 0:
                 stores[-1].append((low, r * per_cell))
+        for copy in spectra.table_copies:
+            copy.wait()
         for index in range(n_basis):
-            spectra.table_copies[index].wait()
             spectra.half(index, stores)
         for target, stage in zip(sorted_bins, stages):
             for i, (center, edge) in enumerate((c, edge) for c, pair in stage for edge in pair):
@@ -279,13 +281,14 @@
 
     hbm, anywhere = (pl.BlockSpec(memory_space=space) for space in (pltpu.HBM, pl.ANY))
     bf16, f32 = jnp.bfloat16, jnp.float32
-    shapes = [((rows - 1) * cols * per_cell, length), (rows * (per_cell + strip), length)]
+    shapes = [((cols - 2) * per_cell, length), ((rows - 1) * cols * per_cell, length)]
+    shapes.append((rows * (per_cell + strip), length))
     shapes = [jax.ShapeDtypeStruct(shape, bf16) for shape in shapes]
     shapes.append(jax.ShapeDtypeStruct((NSEP, 8, per_cell), f32))
     shapes += [jax.ShapeDtypeStruct((size, per_cell, per_cell), bf16) for size in sizes]
     return pl.pallas_call(
         kernel,
-        name="other_rows",
+        name="other_cells",
         out_shape=shapes,
         in_specs=[hbm] * 4 + vmem(1) + [anywhere] + vmem(1),
         out_specs=vmem(len(shapes)),
@@ -398,16 +401,17 @@
     )(*arrays, bins, *carried)
 
 
-def over_mesh(value, axes):
-    for axis in axes:
+def over_mesh(value, ra, dec):
+    def steps(axis):
+        count = lax.axis_size(axis)
+        return [1 << i for i in range(count.bit_length() - 1)]
+
+    exchanges = [(ra, step) for step in steps(ra)] + [(dec, step) for step in steps(dec)[::-1]]
+    for axis, step in exchanges:
         count = lax.axis_size(axis)
         if count & (count - 1):
-            value = lax.psum(value, axis)
-            continue
-        step = 1
-        while step < count:
-            value = value + lax.ppermute(value, axis, [(i, i ^ step) for i in range(count)])
-            step *= 2
+            raise ValueError("axis size")
+        value = value + lax.ppermute(value, axis, [(i, i ^ step) for i in range(count)])
     return value
 
 
@@ -423,12 +427,12 @@
     stages, handed = plan(rows, cols)
     table = dft_table(length, NKB)
     basis = jnp.asarray(table)
-    live = jnp.broadcast_to(block_count[..., None, None], (1, 1, 1, block_pairs.shape[2]))
+    slot = lax.broadcasted_iota(jnp.int32, (1, 1, 1, block_pairs.shape[2]), 3)
+    live = (slot < block_count[..., None, None]).astype(jnp.int32)
     entries = jnp.concatenate([block_pairs.transpose(0, 3, 1, 2), live], axis=1)
-    ends, middle = first_row(forests, pixel_range, resolution, basis)
+    ends = end_cells(forests, pixel_range, resolution, basis)
     above_ends = shifted(ends, "ra", 1)
-    above_middle = shifted(middle, "ra", 1)
-    own, low, counts, *bins = other_rows(
+    middle, own, low, counts, *bins = other_cells(
         forests,
         pixel_range,
         resolution,
@@ -439,6 +443,7 @@
         stages,
         handed,
     )
+    above_middle = shifted(middle, "ra", 1)
     right = shifted(low, "dec", 1)
 
     place = {(0, 0): (0, 0), (0, cols - 1): (0, 1)}
@@ -475,8 +480,9 @@
     partial_too, for_others = sums(1, arrays, given, [])
     from_left = shifted(for_others, "dec", -1)
     own_sums, result = sums(2, arrays, [], [partial, partial_too, counts, for_others])
-    tile_power = ((own_sums + from_left) / (per_cell * length)).reshape(1, 1, NSEP, NKB)
-    total = over_mesh(result, ("dec", "ra"))
+    tile_power = (own_sums + from_left) / (per_cell * length)
+    tile_power = tile_power.reshape(1, 1, NSEP, NKB)
+    total = over_mesh(result, "ra", "dec")
     sky_power = total[:NSEP] / jnp.maximum(total[NSEP:], 1.0)
     return tile_power, sky_power
 

time: 59.9 us -> 61.4 us (1.025)
  the two profiles are of different devices: /device:TPU:0 before, /device:TPU:20 now
where the time goes in v1:
time: 61.4 us; the launch traced here: 61.1 us
  waiting for transfers between devices  23.5 us (38%)
  Pallas kernels  20 us (33%)
  starting transfers between devices  14.2 us (23%)
  other arithmetic  1.91 us (3%)
  between operations  1.54 us (3%)
    pallas_call x3, Pallas kernels, pair_sums(): pl.pallas_call(kernel, out_shape=[jax.ShapeDtypeStruct(shape, jnp.float32...  13.7 us
    ppermute x5, waiting for transfers between devices, shifted(): lax.ppermute(value, axis, [(i + steps, i) for i in range(count) if 0 <= i...  12 us
    ppermute x5, starting transfers between devices, shifted(): lax.ppermute(value, axis, [(i + steps, i) for i in range(count) if 0 <= i...  11.5 us
    ppermute x5, waiting for transfers between devices, over_mesh(): lax.ppermute(value, axis, [(i, i ^ step) for i in range(count)])  11.5 us
    pallas_call x1, Pallas kernels, other_cells(): pl.pallas_call(kernel, name='other_cells', out_shape=shapes, in_specs=[hb...  4.08 us
    ppermute x5, starting transfers between devices, over_mesh(): lax.ppermute(value, axis, [(i, i ^ step) for i in range(count)])  2.64 us
    pallas_call x1, Pallas kernels, end_cells(): pl.pallas_call(kernel, name='end_cells', out_shape=jax.ShapeDtypeStruct((...  2.16 us
  transfers between devices with their start and end apart: 10, of which 7 were waited for; matrix products, arithmetic and copies ran while one was open for 1% of the time, Pallas kernels for 18%

profile of v1, /device:TPU:20, one launch (start us, length us, event | category | flops | bytes accessed | tf_op | source)
XLA Modules:
  0.0 61.1 jit_solution(4737783342391968075)
XLA Ops:
  0.6 0.0 copy-start
  1.4 0.7 %pad_add_fusion.refs_5_ = s32[1,4,1,40]{3,2,1,0:T(1,128)S(1)} fusion(s32[1,1,1,40]{3,2,1,0:T(1,128)S(1)} %compare_convert_fusion, s32[1,3,1,40]{3,2,1,0:T(1,128)} %bitcast.7), kind=kLoop, calls=%fused_computation.3 | loop fusion | flops 160 | bytes 1280 | tf_op jit(solution)/shard_map/concatenate | solution.py:432
  2.1 2.2 %end_cells.1.refs_4_.refs_0_ = bf16[256,1024]{1,0:T(8,128)(2,1)S(1)} custom-call(bf16[2,4,128,1024]{3,2,1,0:T(8,128)(2,1)} %refs_0_.1, s32[2,4,2,128]{3,2,1,0:T(2,128)} %refs_1_.1, f32[2,4,128]{2,1,0:T(4,128)} %refs_2_.1, bf16[2,512,512]{2,1,0:T(8,128)(2,1)} %constant.7.clone.basis.refs_3_), custom_call_target="tpu_custom_call" | custom-call | flops 536870912 | bytes 4194304 | tf_op jit(solution)/shard_map/end_cells/pallas_call | solution.py:206
  4.3 0.0 copy-done
  4.3 4.1 %other_cells.1 = (bf16[256,1024]{1,0:T(8,128)(2,1)S(1)}, bf16[512,1024]{1,0:T(8,128)(2,1)S(1)}, bf16[288,1024]{1,0:T(8,128)(2,1)S(1)}, f32[8,8,128]{2,1,0:T(8,12...) custom-call(bf16[2,4,128,1024]{3,2,1,0:T(8,128)(2,1)} %refs_0_.1, ...), custom_call_target="tpu_custom_call" | custom-call | flops 1610612736 | bytes 8388608 | tf_op jit(solution)/shard_map/other_cells/pallas_call | solution.py:289
  8.4 2.8 %collective-permute-start.3 = (bf16[288,1024]{1,0:T(8,128)(2,1)S(1)}, bf16[288,1024]{1,0:T(8,128)(2,1)S(1)}, u32[]{:S(2)}, u32[]{:S(2)}) collective-permute-start(bf16[288,1024]{1,0:T(8,128)(2,1)S(1)} %get-tuple-element.21), channel_id=1, source_target_pairs={{1,0},{2,1},{3,2},{4,3},{5,4},{6,5},{7,6},{9,8},{10,9},{11,10},{12... | collective-permute-start | bytes 1769480 | tf_op jit(solution)/shard_map/ppermute | solution.py:420
  11.2 2.4 %collective-permute-start = (bf16[256,1024]{1,0:T(8,128)(2,1)S(1)}, bf16[256,1024]{1,0:T(8,128)(2,1)S(1)}, u32[]{:S(2)}, u32[]{:S(2)}) collective-permute-start(bf16[256,1024]{1,0:T(8,128)(2,1)S(1)} %end_cells.1.refs_4_.refs_0_), channel_id=1, source_target_pairs={{8,0},{16,8},{24,16},{9,1},{17,9},{25,17},{10,2},{18,10},{26,18},{... | collective-permute-start | bytes 1572872 | tf_op jit(solution)/shard_map/ppermute | solution.py:420
  13.6 2.4 %collective-permute-start.1 = (bf16[256,1024]{1,0:T(8,128)(2,1)S(1)}, bf16[256,1024]{1,0:T(8,128)(2,1)S(1)}, u32[]{:S(2)}, u32[]{:S(2)}) collective-permute-start(bf16[256,1024]{1,0:T(8,128)(2,1)S(1)} %get-tuple-element.16.refs_1_), channel_id=1, source_target_pairs={{8,0},{16,8},{24,16},{9,1},{17,9},{25,17},{10,2},{18,10},{26,18},{... | collective-permute-start | bytes 1572872 | tf_op jit(solution)/shard_map/ppermute | solution.py:420
  15.9 6.9 %shard_map.86.refs_5_ = f32[2,8,8,128]{3,2,1,0:T(8,128)S(1)} custom-call(bf16[256,1024]{1,0:T(8,128)(2,1)S(1)} %end_cells.1.refs_4_.refs_0_, bf16[256,1024]{1,0:T(8,128)(2,1)S(1)} %get-tuple-element.16.refs_1_, bf16[512,1024]{1,0:T(8,128)(2,1)S(1)} %get-tuple-element.15.refs_2_.refs_1_.refs_0_, bf16[22,128,128]{2,1,0:T(8,128)(2,1)S(1)} %get-tuple-element.17.refs_3_), custom_call_target="tpu_custom_call" | custom-call | flops 5905580032 | bytes 1048576 | tf_op jit(solution)/shard_map/pallas_call | solution.py:393
  22.9 5.0 %collective-permute-done.refs_3_.refs_1_ = bf16[256,1024]{1,0:T(8,128)(2,1)S(1)} collective-permute-done((bf16[256,1024]{1,0:T(8,128)(2,1)S(1)}, bf16[256,1024]{1,0:T(8,128)(2,1)S(1)}, u32[]{:S(2)}, u32[]{:S(2)}) %collective-permute-start) | collective-permute-done | bytes 524320 | tf_op jit(solution)/shard_map/ppermute | solution.py:420
  27.9 2.1 %collective-permute-start.2 = (bf16[128,1024]{1,0:T(8,128)(2,1)S(1)}, bf16[128,1024]{1,0:T(8,128)(2,1)S(1)}, u32[]{:S(2)}, u32[]{:S(2)}) collective-permute-start(bf16[128,1024]{1,0:T(8,128)(2,1)S(1)} %slice.9), channel_id=1, source_target_pairs={{1,0},{2,1},{3,2},{4,3},{5,4},{6,5},{7,6},{9,8},{10,9},{11,10},{12... | collective-permute-start | bytes 786440 | tf_op jit(solution)/shard_map/ppermute | solution.py:420
  30.0 0.0 collective-permute-done.3.refs_2_
  30.0 4.0 %shard_map.87 = (f32[2,8,8,128]{3,2,1,0:T(8,128)S(1)}, f32[8,128]{1,0:T(8,128)S(1)}) custom-call(bf16[256,1024]{1,0:T(8,128)(2,1)S(1)} %end_cells.1.refs_4_.refs_0_, bf16[512,1024]{1,0:T(8,128)(2,1)S(1)} %get-tuple-element.15.refs_2_.refs_1_.refs_0_, bf16[288,1024]{1,0:T(8,128)(2,1)S(1)} %collective-permute-done.3.refs_2_, ...), custom_call_target="tpu_custom_call" | custom-call | flops 2684354560 | bytes 1048576 | tf_op jit(solution)/shard_map/pallas_call | solution.py:393
  34.0 3.8 %collective-permute-done.1.refs_2_ = bf16[256,1024]{1,0:T(8,128)(2,1)S(1)} collective-permute-done((bf16[256,1024]{1,0:T(8,128)(2,1)S(1)}, bf16[256,1024]{1,0:T(8,128)(2,1)S(1)}, u32[]{:S(2)}, u32[]{:S(2)}) %collective-permute-start.1) | collective-permute-done | bytes 524320 | tf_op jit(solution)/shard_map/ppermute | solution.py:420
  37.8 0.0 collective-permute-done.2.refs_3_
  37.8 2.8 %shard_map.88 = (f32[8,128]{1,0:T(8,128)S(1)}, f32[16,128]{1,0:T(8,128)S(1)}) custom-call(bf16[512,1024]{1,0:T(8,128)(2,1)S(1)} %get-tuple-element.15.refs_2_.refs_1_.refs_0_, bf16[256,1024]{1,0:T(8,128)(2,1)S(1)} %collective-permute-done.refs_3_.refs_1_, bf16[256,1024]{1,0:T(8,128)(2,1)S(1)} %collective-permute-done.1.refs_2_, ...), custom_call_target="tpu_custom_call" | custom-call | flops 2147483648 | bytes 1048576 | tf_op jit(solution)/shard_map/pallas_call | solution.py:393
  40.6 0.1 collective-permute-start.5
  40.7 3.6 %collective-permute-done.5 = f32[16,128]{1,0:T(8,128)S(1)} collective-permute-done((f32[16,128]{1,0:T(8,128)S(1)}, f32[16,128]{1,0:T(8,128)S(1)}, u32[]{:S(2)}, u32[]{:S(2)}) %collective-permute-start.5) | collective-permute-done | bytes 8224 | tf_op jit(solution)/shard_map/ppermute | solution.py:414
  44.3 0.4 collective-permute-start.6
  44.7 4.2 %collective-permute-done.6 = f32[16,128]{1,0:T(8,128)S(1)} collective-permute-done((f32[16,128]{1,0:T(8,128)S(1)}, f32[16,128]{1,0:T(8,128)S(1)}, u32[]{:S(2)}, u32[]{:S(2)}) %collective-permute-start.6) | collective-permute-done | bytes 8224 | tf_op jit(solution)/shard_map/ppermute | solution.py:414
  48.9 0.2 collective-permute-start.7
  49.1 3.4 %collective-permute-done.7 = f32[16,128]{1,0:T(8,128)S(1)} collective-permute-done((f32[16,128]{1,0:T(8,128)S(1)}, f32[16,128]{1,0:T(8,128)S(1)}, u32[]{:S(2)}, u32[]{:S(2)}) %collective-permute-start.7) | collective-permute-done | bytes 8224 | tf_op jit(solution)/shard_map/ppermute | solution.py:414
  52.6 1.5 %collective-permute-start.8 = (f32[16,128]{1,0:T(8,128)S(1)}, f32[16,128]{1,0:T(8,128)S(1)}, u32[]{:S(2)}, u32[]{:S(2)}) collective-permute-start(f32[16,128]{1,0:T(8,128)S(1)} %add.21), channel_id=1, source_target_pairs={{0,2},{1,3},{2,0},{3,1},{4,6},{5,7},{6,4},{7,5},{8,10},{9,11},{10,... | collective-permute-start | bytes 24584 | tf_op jit(solution)/shard_map/ppermute | solution.py:414
  54.1 1.9 %collective-permute-start.4 = (f32[8,128]{1,0:T(8,128)S(1)}, f32[8,128]{1,0:T(8,128)S(1)}, u32[]{:S(2)}, u32[]{:S(2)}) collective-permute-start(f32[8,128]{1,0:T(8,128)S(1)} %get-tuple-element.25.refs_8_), channel_id=1, source_target_pairs={{0,1},{1,2},{2,3},{3,4},{4,5},{5,6},{6,7},{8,9},{9,10},{10,11},{11... | collective-permute-start | bytes 12296 | tf_op jit(solution)/shard_map/ppermute | solution.py:420
  56.0 0.2 collective-permute-done.8
  56.2 0.5 collective-permute-start.9
  56.7 3.2 %collective-permute-done.4 = f32[8,128]{1,0:T(8,128)S(1)} collective-permute-done((f32[8,128]{1,0:T(8,128)S(1)}, f32[8,128]{1,0:T(8,128)S(1)}, u32[]{:S(2)}, u32[]{:S(2)}) %collective-permute-start.4) | collective-permute-done | bytes 4128 | tf_op jit(solution)/shard_map/ppermute | solution.py:420
  59.9 0.6 multiply_bitcast_fusion
  60.5 0.0 collective-permute-done.9
  60.5 0.6 fusion
  (7 shorter events, 0.0 us)
Async XLA Ops:
  0.6 3.7 %copy-start = (s32[1,1,40,128,128]{4,3,2,1,0:T(8,128)S(1)}, s32[1,1,40,128,128]{4,3,2,1,0:T(8,128)}, u32[]{:S(2)}) copy-start(s32[1,1,40,128,128]{4,3,2,1,0:T(8,128)} %param.12) | copy-start | bytes 7864324
  8.4 21.6 %collective-permute-start.3 = (bf16[288,1024]{1,0:T(8,128)(2,1)S(1)}, bf16[288,1024]{1,0:T(8,128)(2,1)S(1)}, u32[]{:S(2)}, u32[]{:S(2)}) collective-permute-start(bf16[288,1024]{1,0:T(8,128)(2,1)S(1)} %get-tuple-element.21), channel_id=1, source_target_pairs={{1,0},{2,1},{3,2},{4,3},{5,4},{6,5},{7,6},{9,8},{10,9},{11,10},{12... | collective-permute-start | bytes 1769480 | tf_op jit(solution)/shard_map/ppermute | solution.py:420
  11.2 16.7 %collective-permute-start = (bf16[256,1024]{1,0:T(8,128)(2,1)S(1)}, bf16[256,1024]{1,0:T(8,128)(2,1)S(1)}, u32[]{:S(2)}, u32[]{:S(2)}) collective-permute-start(bf16[256,1024]{1,0:T(8,128)(2,1)S(1)} %end_cells.1.refs_4_.refs_0_), channel_id=1, source_target_pairs={{8,0},{16,8},{24,16},{9,1},{17,9},{25,17},{10,2},{18,10},{26,18},{... | collective-permute-start | bytes 1572872 | tf_op jit(solution)/shard_map/ppermute | solution.py:420
  13.6 24.2 %collective-permute-start.1 = (bf16[256,1024]{1,0:T(8,128)(2,1)S(1)}, bf16[256,1024]{1,0:T(8,128)(2,1)S(1)}, u32[]{:S(2)}, u32[]{:S(2)}) collective-permute-start(bf16[256,1024]{1,0:T(8,128)(2,1)S(1)} %get-tuple-element.16.refs_1_), channel_id=1, source_target_pairs={{8,0},{16,8},{24,16},{9,1},{17,9},{25,17},{10,2},{18,10},{26,18},{... | collective-permute-start | bytes 1572872 | tf_op jit(solution)/shard_map/ppermute | solution.py:420
  27.9 9.9 %collective-permute-start.2 = (bf16[128,1024]{1,0:T(8,128)(2,1)S(1)}, bf16[128,1024]{1,0:T(8,128)(2,1)S(1)}, u32[]{:S(2)}, u32[]{:S(2)}) collective-permute-start(bf16[128,1024]{1,0:T(8,128)(2,1)S(1)} %slice.9), channel_id=1, source_target_pairs={{1,0},{2,1},{3,2},{4,3},{5,4},{6,5},{7,6},{9,8},{10,9},{11,10},{12... | collective-permute-start | bytes 786440 | tf_op jit(solution)/shard_map/ppermute | solution.py:420
  40.6 3.7 %collective-permute-start.5 = (f32[16,128]{1,0:T(8,128)S(1)}, f32[16,128]{1,0:T(8,128)S(1)}, u32[]{:S(2)}, u32[]{:S(2)}) collective-permute-start(f32[16,128]{1,0:T(8,128)S(1)} %get-tuple-element.27), channel_id=1, source_target_pairs={{0,8},{8,0},{16,24},{24,16},{1,9},{9,1},{17,25},{25,17},{2,10},{10... | collective-permute-start | bytes 24584 | tf_op jit(solution)/shard_map/ppermute | solution.py:414
  44.3 4.5 %collective-permute-start.6 = (f32[16,128]{1,0:T(8,128)S(1)}, f32[16,128]{1,0:T(8,128)S(1)}, u32[]{:S(2)}, u32[]{:S(2)}) collective-permute-start(f32[16,128]{1,0:T(8,128)S(1)} %add.19), channel_id=1, source_target_pairs={{0,16},{8,24},{16,0},{24,8},{1,17},{9,25},{17,1},{25,9},{2,18},{10... | collective-permute-start | bytes 24584 | tf_op jit(solution)/shard_map/ppermute | solution.py:414
  48.9 3.7 %collective-permute-start.7 = (f32[16,128]{1,0:T(8,128)S(1)}, f32[16,128]{1,0:T(8,128)S(1)}, u32[]{:S(2)}, u32[]{:S(2)}) collective-permute-start(f32[16,128]{1,0:T(8,128)S(1)} %add.20), channel_id=1, source_target_pairs={{0,4},{1,5},{2,6},{3,7},{4,0},{5,1},{6,2},{7,3},{8,12},{9,13},{10,... | collective-permute-start | bytes 24584 | tf_op jit(solution)/shard_map/ppermute | solution.py:414
  52.6 3.7 %collective-permute-start.8 = (f32[16,128]{1,0:T(8,128)S(1)}, f32[16,128]{1,0:T(8,128)S(1)}, u32[]{:S(2)}, u32[]{:S(2)}) collective-permute-start(f32[16,128]{1,0:T(8,128)S(1)} %add.21), channel_id=1, source_target_pairs={{0,2},{1,3},{2,0},{3,1},{4,6},{5,7},{6,4},{7,5},{8,10},{9,11},{10,... | collective-permute-start | bytes 24584 | tf_op jit(solution)/shard_map/ppermute | solution.py:414
  54.1 5.8 %collective-permute-start.4 = (f32[8,128]{1,0:T(8,128)S(1)}, f32[8,128]{1,0:T(8,128)S(1)}, u32[]{:S(2)}, u32[]{:S(2)}) collective-permute-start(f32[8,128]{1,0:T(8,128)S(1)} %get-tuple-element.25.refs_8_), channel_id=1, source_target_pairs={{0,1},{1,2},{2,3},{3,4},{4,5},{5,6},{6,7},{8,9},{9,10},{10,11},{11... | collective-permute-start | bytes 12296 | tf_op jit(solution)/shard_map/ppermute | solution.py:420
  56.2 4.3 %collective-permute-start.9 = (f32[16,128]{1,0:T(8,128)S(1)}, f32[16,128]{1,0:T(8,128)S(1)}, u32[]{:S(2)}, u32[]{:S(2)}) collective-permute-start(f32[16,128]{1,0:T(8,128)S(1)} %add.22), channel_id=1, source_target_pairs={{0,1},{1,0},{2,3},{3,2},{4,5},{5,4},{6,7},{7,6},{8,9},{9,8},{10,11... | collective-permute-start | bytes 24584 | tf_op jit(solution)/shard_map/ppermute | solution.py:414

commit v2 on v1

--- a/solution.py
+++ b/solution.py
@@ -401,18 +401,26 @@
     )(*arrays, bins, *carried)
 
 
-def over_mesh(value, ra, dec):
-    def steps(axis):
+def over_mesh(value, extra):
+    n_ra, n_dec = lax.axis_size("ra"), lax.axis_size("dec")
+    if n_dec < 4 or n_dec & (n_dec - 1) or n_ra & (n_ra - 1):
+        return lax.psum(value, ("ra", "dec")), shifted(extra, "dec", -1)
+    along_ra = [("ra", 1 << k) for k in range(n_ra.bit_length() - 1)]
+    along_dec = [("dec", 1 << k) for k in range(1, n_dec.bit_length() - 1)]
+    size, here = value.shape[0], lax.axis_index("dec")
+    passed = from_left = extra
+    for axis, step in [*along_ra[:1], ("dec", 1), *along_dec, *along_ra[1:]]:
+        mask = 3 if (axis, step) == ("dec", 2) else step
+        message = value
+        if axis == "dec":
+            message = jnp.concatenate([value, extra if step == 1 else passed], axis=0)
         count = lax.axis_size(axis)
-        return [1 << i for i in range(count.bit_length() - 1)]
-
-    exchanges = [(ra, step) for step in steps(ra)] + [(dec, step) for step in steps(dec)[::-1]]
-    for axis, step in exchanges:
-        count = lax.axis_size(axis)
-        if count & (count - 1):
-            raise ValueError("axis size")
-        value = value + lax.ppermute(value, axis, [(i, i ^ step) for i in range(count)])
-    return value
+        other = lax.ppermute(message, axis, [(i, i ^ mask) for i in range(count)])
+        value = value + other[:size]
+        if axis == "dec":
+            from_left = jnp.where(here % (2 * step) == step, other[size:], from_left)
+            passed = passed if step == 1 else other[size:]
+    return value, jnp.where(here == 0, jnp.zeros_like(from_left), from_left)
 
 
 def shifted(value, axis, steps):
@@ -478,11 +486,9 @@
     arrays[4] = above_ends
     arrays.append(shifted(above_ends[:per_cell], "dec", 1))
     partial_too, for_others = sums(1, arrays, given, [])
-    from_left = shifted(for_others, "dec", -1)
     own_sums, result = sums(2, arrays, [], [partial, partial_too, counts, for_others])
-    tile_power = (own_sums + from_left) / (per_cell * length)
-    tile_power = tile_power.reshape(1, 1, NSEP, NKB)
-    total = over_mesh(result, "ra", "dec")
+    total, from_left = over_mesh(result, for_others)
+    tile_power = ((own_sums + from_left) / (per_cell * length)).reshape(1, 1, NSEP, NKB)
     sky_power = total[:NSEP] / jnp.maximum(total[NSEP:], 1.0)
     return tile_power, sky_power
 

time: 61.4 us -> 58.9 us (0.959)
  the two profiles are of different devices: /device:TPU:20 before, /device:TPU:0 now
where the time goes in v2:
time: 58.9 us; the launch traced here: 58.6 us
  waiting for transfers between devices  20.6 us (35%)
  Pallas kernels  20 us (34%)
  starting transfers between devices  14.5 us (25%)
  other arithmetic  1.93 us (3%)
  between operations  1.53 us (3%)
    pallas_call x3, Pallas kernels, pair_sums(): pl.pallas_call(kernel, out_shape=[jax.ShapeDtypeStruct(shape, jnp.float32...  13.7 us
    ppermute x4, waiting for transfers between devices, shifted(): lax.ppermute(value, axis, [(i + steps, i) for i in range(count) if 0 <= i...  13.5 us
    ppermute x5, starting transfers between devices, over_mesh(): other = lax.ppermute(message, axis, [(i, i ^ mask) for i in range(count)])  9.17 us
    ppermute x5, waiting for transfers between devices, over_mesh(): other = lax.ppermute(message, axis, [(i, i ^ mask) for i in range(count)])  7.12 us
    ppermute x4, starting transfers between devices, shifted(): lax.ppermute(value, axis, [(i + steps, i) for i in range(count) if 0 <= i...  5.35 us
    pallas_call x1, Pallas kernels, other_cells(): pl.pallas_call(kernel, name='other_cells', out_shape=shapes, in_specs=[hb...  4.09 us
    pallas_call x1, Pallas kernels, end_cells(): pl.pallas_call(kernel, name='end_cells', out_shape=jax.ShapeDtypeStruct((...  2.17 us
  transfers between devices with their start and end apart: 9, of which 7 were waited for; matrix products, arithmetic and copies ran while one was open for 1% of the time, Pallas kernels for 19%

profile of v2, /device:TPU:0, one launch (start us, length us, event | category | flops | bytes accessed | tf_op | source)
XLA Modules:
  0.0 58.6 jit_solution(3373068366055682800)
XLA Ops:
  0.6 0.0 copy-start
  1.4 0.7 %pad_add_fusion.refs_5_ = s32[1,4,1,40]{3,2,1,0:T(1,128)S(1)} fusion(s32[1,1,1,40]{3,2,1,0:T(1,128)S(1)} %compare_convert_fusion, s32[1,3,1,40]{3,2,1,0:T(1,128)} %bitcast.7), kind=kLoop, calls=%fused_computation.15 | loop fusion | flops 160 | bytes 1280 | tf_op jit(solution)/shard_map/concatenate | solution.py:440
  2.1 2.2 %end_cells.1.refs_4_.refs_0_ = bf16[256,1024]{1,0:T(8,128)(2,1)S(1)} custom-call(bf16[2,4,128,1024]{3,2,1,0:T(8,128)(2,1)} %refs_0_.1, s32[2,4,2,128]{3,2,1,0:T(2,128)} %refs_1_.1, f32[2,4,128]{2,1,0:T(4,128)} %refs_2_.1, bf16[2,512,512]{2,1,0:T(8,128)(2,1)} %constant.48.clone.basis.refs_3_), custom_call_target="tpu_custom_call" | custom-call | flops 536870912 | bytes 4194304 | tf_op jit(solution)/shard_map/end_cells/pallas_call | solution.py:206
  4.3 0.0 copy-done
  4.3 4.1 %other_cells.1 = (bf16[256,1024]{1,0:T(8,128)(2,1)S(1)}, bf16[512,1024]{1,0:T(8,128)(2,1)S(1)}, bf16[288,1024]{1,0:T(8,128)(2,1)S(1)}, f32[8,8,128]{2,1,0:T(8,12...) custom-call(bf16[2,4,128,1024]{3,2,1,0:T(8,128)(2,1)} %refs_0_.1, ...), custom_call_target="tpu_custom_call" | custom-call | flops 1610612736 | bytes 8388608 | tf_op jit(solution)/shard_map/other_cells/pallas_call | solution.py:289
  8.4 1.3 %collective-permute-start.3 = (bf16[288,1024]{1,0:T(8,128)(2,1)S(1)}, bf16[288,1024]{1,0:T(8,128)(2,1)S(1)}, u32[]{:S(2)}, u32[]{:S(2)}) collective-permute-start(bf16[288,1024]{1,0:T(8,128)(2,1)S(1)} %get-tuple-element.21), channel_id=1, source_target_pairs={{1,0},{2,1},{3,2},{4,3},{5,4},{6,5},{7,6},{9,8},{10,9},{11,10},{12... | collective-permute-start | bytes 1769480 | tf_op jit(solution)/shard_map/ppermute | solution.py:428
  9.7 1.3 %collective-permute-start = (bf16[256,1024]{1,0:T(8,128)(2,1)S(1)}, bf16[256,1024]{1,0:T(8,128)(2,1)S(1)}, u32[]{:S(2)}, u32[]{:S(2)}) collective-permute-start(bf16[256,1024]{1,0:T(8,128)(2,1)S(1)} %end_cells.1.refs_4_.refs_0_), channel_id=1, source_target_pairs={{8,0},{16,8},{24,16},{9,1},{17,9},{25,17},{10,2},{18,10},{26,18},{... | collective-permute-start | bytes 1572872 | tf_op jit(solution)/shard_map/ppermute | solution.py:428
  11.0 1.3 %collective-permute-start.1 = (bf16[256,1024]{1,0:T(8,128)(2,1)S(1)}, bf16[256,1024]{1,0:T(8,128)(2,1)S(1)}, u32[]{:S(2)}, u32[]{:S(2)}) collective-permute-start(bf16[256,1024]{1,0:T(8,128)(2,1)S(1)} %get-tuple-element.16.refs_1_), channel_id=1, source_target_pairs={{8,0},{16,8},{24,16},{9,1},{17,9},{25,17},{10,2},{18,10},{26,18},{... | collective-permute-start | bytes 1572872 | tf_op jit(solution)/shard_map/ppermute | solution.py:428
  12.3 6.9 %shard_map.86.refs_5_ = f32[2,8,8,128]{3,2,1,0:T(8,128)S(1)} custom-call(bf16[256,1024]{1,0:T(8,128)(2,1)S(1)} %end_cells.1.refs_4_.refs_0_, bf16[256,1024]{1,0:T(8,128)(2,1)S(1)} %get-tuple-element.16.refs_1_, bf16[512,1024]{1,0:T(8,128)(2,1)S(1)} %get-tuple-element.15.refs_2_.refs_1_.refs_0_, bf16[22,128,128]{2,1,0:T(8,128)(2,1)S(1)} %get-tuple-element.17.refs_3_), custom_call_target="tpu_custom_call" | custom-call | flops 5905580032 | bytes 1048576 | tf_op jit(solution)/shard_map/pallas_call | solution.py:393
  19.3 7.7 %collective-permute-done.refs_3_.refs_1_ = bf16[256,1024]{1,0:T(8,128)(2,1)S(1)} collective-permute-done((bf16[256,1024]{1,0:T(8,128)(2,1)S(1)}, bf16[256,1024]{1,0:T(8,128)(2,1)S(1)}, u32[]{:S(2)}, u32[]{:S(2)}) %collective-permute-start) | collective-permute-done | bytes 524320 | tf_op jit(solution)/shard_map/ppermute | solution.py:428
  27.0 1.5 %collective-permute-start.2 = (bf16[128,1024]{1,0:T(8,128)(2,1)S(1)}, bf16[128,1024]{1,0:T(8,128)(2,1)S(1)}, u32[]{:S(2)}, u32[]{:S(2)}) collective-permute-start(bf16[128,1024]{1,0:T(8,128)(2,1)S(1)} %slice.28), channel_id=1, source_target_pairs={{1,0},{2,1},{3,2},{4,3},{5,4},{6,5},{7,6},{9,8},{10,9},{11,10},{12... | collective-permute-start | bytes 786440 | tf_op jit(solution)/shard_map/ppermute | solution.py:428
  28.5 0.0 collective-permute-done.3.refs_2_
  28.5 4.0 %shard_map.87 = (f32[2,8,8,128]{3,2,1,0:T(8,128)S(1)}, f32[8,128]{1,0:T(8,128)S(1)}) custom-call(bf16[256,1024]{1,0:T(8,128)(2,1)S(1)} %end_cells.1.refs_4_.refs_0_, bf16[512,1024]{1,0:T(8,128)(2,1)S(1)} %get-tuple-element.15.refs_2_.refs_1_.refs_0_, bf16[288,1024]{1,0:T(8,128)(2,1)S(1)} %collective-permute-done.3.refs_2_, ...), custom_call_target="tpu_custom_call" | custom-call | flops 2684354560 | bytes 1048576 | tf_op jit(solution)/shard_map/pallas_call | solution.py:393
  32.5 5.7 %collective-permute-done.1.refs_2_ = bf16[256,1024]{1,0:T(8,128)(2,1)S(1)} collective-permute-done((bf16[256,1024]{1,0:T(8,128)(2,1)S(1)}, bf16[256,1024]{1,0:T(8,128)(2,1)S(1)}, u32[]{:S(2)}, u32[]{:S(2)}) %collective-permute-start.1) | collective-permute-done | bytes 524320 | tf_op jit(solution)/shard_map/ppermute | solution.py:428
  38.2 0.0 collective-permute-done.2.refs_3_
  38.2 2.8 %shard_map.88 = (f32[8,128]{1,0:T(8,128)S(1)}, f32[16,128]{1,0:T(8,128)S(1)}) custom-call(bf16[512,1024]{1,0:T(8,128)(2,1)S(1)} %get-tuple-element.15.refs_2_.refs_1_.refs_0_, bf16[256,1024]{1,0:T(8,128)(2,1)S(1)} %collective-permute-done.refs_3_.refs_1_, bf16[256,1024]{1,0:T(8,128)(2,1)S(1)} %collective-permute-done.1.refs_2_, ...), custom_call_target="tpu_custom_call" | custom-call | flops 2147483648 | bytes 1048576 | tf_op jit(solution)/shard_map/pallas_call | solution.py:393
  41.1 2.4 %collective-permute-start.4 = (f32[16,128]{1,0:T(8,128)S(1)}, f32[16,128]{1,0:T(8,128)S(1)}, u32[]{:S(2)}, u32[]{:S(2)}) collective-permute-start(f32[16,128]{1,0:T(8,128)S(1)} %get-tuple-element.27), channel_id=1, source_target_pairs={{0,8},{8,0},{16,24},{24,16},{1,9},{9,1},{17,25},{25,17},{2,10},{10... | collective-permute-start | bytes 24584 | tf_op jit(solution)/shard_map/ppermute | solution.py:418
  43.4 1.6 %collective-permute-done.4 = f32[16,128]{1,0:T(8,128)S(1)} collective-permute-done((f32[16,128]{1,0:T(8,128)S(1)}, f32[16,128]{1,0:T(8,128)S(1)}, u32[]{:S(2)}, u32[]{:S(2)}) %collective-permute-start.4) | collective-permute-done | bytes 8224 | tf_op jit(solution)/shard_map/ppermute | solution.py:418
  45.1 0.0 collective-permute-start.5
  45.1 1.2 %collective-permute-done.5 = f32[24,128]{1,0:T(8,128)S(1)} collective-permute-done((f32[24,128]{1,0:T(8,128)S(1)}, f32[24,128]{1,0:T(8,128)S(1)}, u32[]{:S(2)}, u32[]{:S(2)}) %collective-permute-start.5) | collective-permute-done | bytes 12320 | tf_op jit(solution)/shard_map/ppermute | solution.py:418
  46.3 2.0 %collective-permute-start.6 = (f32[24,128]{1,0:T(8,128)S(1)}, f32[24,128]{1,0:T(8,128)S(1)}, u32[]{:S(2)}, u32[]{:S(2)}) collective-permute-start(f32[24,128]{1,0:T(8,128)S(1)} %pad_maximum_fusion), channel_id=1, source_target_pairs={{0,3},{1,2},{2,1},{3,0},{4,7},{5,6},{6,5},{7,4},{8,11},{9,10},{10,... | collective-permute-start | bytes 36872 | tf_op jit(solution)/shard_map/ppermute | solution.py:418
  48.3 1.4 %collective-permute-done.6 = f32[24,128]{1,0:T(8,128)S(1)} collective-permute-done((f32[24,128]{1,0:T(8,128)S(1)}, f32[24,128]{1,0:T(8,128)S(1)}, u32[]{:S(2)}, u32[]{:S(2)}) %collective-permute-start.6) | collective-permute-done | bytes 12320 | tf_op jit(solution)/shard_map/ppermute | solution.py:418
  49.7 2.0 %collective-permute-start.7 = (f32[24,128]{1,0:T(8,128)S(1)}, f32[24,128]{1,0:T(8,128)S(1)}, u32[]{:S(2)}, u32[]{:S(2)}) collective-permute-start(f32[24,128]{1,0:T(8,128)S(1)} %pad_maximum_fusion.2), channel_id=1, source_target_pairs={{0,4},{1,5},{2,6},{3,7},{4,0},{5,1},{6,2},{7,3},{8,12},{9,13},{10,... | collective-permute-start | bytes 36872 | tf_op jit(solution)/shard_map/ppermute | solution.py:418
  51.7 1.7 %collective-permute-done.7 = f32[24,128]{1,0:T(8,128)S(1)} collective-permute-done((f32[24,128]{1,0:T(8,128)S(1)}, f32[24,128]{1,0:T(8,128)S(1)}, u32[]{:S(2)}, u32[]{:S(2)}) %collective-permute-start.7) | collective-permute-done | bytes 12320 | tf_op jit(solution)/shard_map/ppermute | solution.py:418
  53.5 2.7 %collective-permute-start.8 = (f32[16,128]{1,0:T(8,128)S(1)}, f32[16,128]{1,0:T(8,128)S(1)}, u32[]{:S(2)}, u32[]{:S(2)}) collective-permute-start(f32[16,128]{1,0:T(8,128)S(1)} %slice_add_fusion), channel_id=1, source_target_pairs={{0,16},{8,24},{16,0},{24,8},{1,17},{9,25},{17,1},{25,9},{2,18},{10... | collective-permute-start | bytes 24584 | tf_op jit(solution)/shard_map/ppermute | solution.py:418
  56.2 0.6 %fusion.6 = f32[1,1,8,128]{3,2,1,0:T(8,128)} fusion(f32[8,128]{1,0:T(8,128)S(1)} %get-tuple-element.26, f32[8,128]{1,0:T(8,128)S(1)} %get-tuple-element.25.refs_8_, f32[24,128]{1,0:T(8,128)S(1)} %collective-permute-done.5, f32[24,128]{1,0:T(8,128)S(1)} %collective-permute-done.7, pred[]{:T(512)S(6)} %eq.19, pred[]{:T(512)S(6)} %eq.18, pred[]{:T(512)S(6)} %eq.17, ...), kind=kLoop, calls=%fused_computation.14 | loop fusion | flops 6144 | bytes 24580 | tf_op jit(solution)/shard_map/reshape | solution.py:491
  56.8 1.2 %collective-permute-done.8 = f32[16,128]{1,0:T(8,128)S(1)} collective-permute-done((f32[16,128]{1,0:T(8,128)S(1)}, f32[16,128]{1,0:T(8,128)S(1)}, u32[]{:S(2)}, u32[]{:S(2)}) %collective-permute-start.8) | collective-permute-done | bytes 8224 | tf_op jit(solution)/shard_map/ppermute | solution.py:418
  58.0 0.6 %fusion = f32[8,128]{1,0:T(8,128)} fusion(f32[16,128]{1,0:T(8,128)S(1)} %add.36), kind=kLoop, calls=%fused_computation.7 | loop fusion | flops 2048 | bytes 12288 | tf_op jit(solution)/shard_map/div | solution.py:492
  (11 shorter events, 0.1 us)
Async XLA Ops:
  0.6 3.7 %copy-start = (s32[1,1,40,128,128]{4,3,2,1,0:T(8,128)S(1)}, s32[1,1,40,128,128]{4,3,2,1,0:T(8,128)}, u32[]{:S(2)}) copy-start(s32[1,1,40,128,128]{4,3,2,1,0:T(8,128)} %param.12) | copy-start | bytes 7864324
  8.4 20.1 %collective-permute-start.3 = (bf16[288,1024]{1,0:T(8,128)(2,1)S(1)}, bf16[288,1024]{1,0:T(8,128)(2,1)S(1)}, u32[]{:S(2)}, u32[]{:S(2)}) collective-permute-start(bf16[288,1024]{1,0:T(8,128)(2,1)S(1)} %get-tuple-element.21), channel_id=1, source_target_pairs={{1,0},{2,1},{3,2},{4,3},{5,4},{6,5},{7,6},{9,8},{10,9},{11,10},{12... | collective-permute-start | bytes 1769480 | tf_op jit(solution)/shard_map/ppermute | solution.py:428
  9.7 17.3 %collective-permute-start = (bf16[256,1024]{1,0:T(8,128)(2,1)S(1)}, bf16[256,1024]{1,0:T(8,128)(2,1)S(1)}, u32[]{:S(2)}, u32[]{:S(2)}) collective-permute-start(bf16[256,1024]{1,0:T(8,128)(2,1)S(1)} %end_cells.1.refs_4_.refs_0_), channel_id=1, source_target_pairs={{8,0},{16,8},{24,16},{9,1},{17,9},{25,17},{10,2},{18,10},{26,18},{... | collective-permute-start | bytes 1572872 | tf_op jit(solution)/shard_map/ppermute | solution.py:428
  11.0 27.2 %collective-permute-start.1 = (bf16[256,1024]{1,0:T(8,128)(2,1)S(1)}, bf16[256,1024]{1,0:T(8,128)(2,1)S(1)}, u32[]{:S(2)}, u32[]{:S(2)}) collective-permute-start(bf16[256,1024]{1,0:T(8,128)(2,1)S(1)} %get-tuple-element.16.refs_1_), channel_id=1, source_target_pairs={{8,0},{16,8},{24,16},{9,1},{17,9},{25,17},{10,2},{18,10},{26,18},{... | collective-permute-start | bytes 1572872 | tf_op jit(solution)/shard_map/ppermute | solution.py:428
  27.0 11.2 %collective-permute-start.2 = (bf16[128,1024]{1,0:T(8,128)(2,1)S(1)}, bf16[128,1024]{1,0:T(8,128)(2,1)S(1)}, u32[]{:S(2)}, u32[]{:S(2)}) collective-permute-start(bf16[128,1024]{1,0:T(8,128)(2,1)S(1)} %slice.28), channel_id=1, source_target_pairs={{1,0},{2,1},{3,2},{4,3},{5,4},{6,5},{7,6},{9,8},{10,9},{11,10},{12... | collective-permute-start | bytes 786440 | tf_op jit(solution)/shard_map/ppermute | solution.py:428
  41.1 4.0 %collective-permute-start.4 = (f32[16,128]{1,0:T(8,128)S(1)}, f32[16,128]{1,0:T(8,128)S(1)}, u32[]{:S(2)}, u32[]{:S(2)}) collective-permute-start(f32[16,128]{1,0:T(8,128)S(1)} %get-tuple-element.27), channel_id=1, source_target_pairs={{0,8},{8,0},{16,24},{24,16},{1,9},{9,1},{17,25},{25,17},{2,10},{10... | collective-permute-start | bytes 24584 | tf_op jit(solution)/shard_map/ppermute | solution.py:418
  45.1 1.2 %collective-permute-start.5 = (f32[24,128]{1,0:T(8,128)S(1)}, f32[24,128]{1,0:T(8,128)S(1)}, u32[]{:S(2)}, u32[]{:S(2)}) collective-permute-start(f32[24,128]{1,0:T(8,128)S(1)} %pad_maximum_fusion.1), channel_id=1, source_target_pairs={{0,1},{1,0},{2,3},{3,2},{4,5},{5,4},{6,7},{7,6},{8,9},{9,8},{10,11... | collective-permute-start | bytes 36872 | tf_op jit(solution)/shard_map/ppermute | solution.py:418
  46.3 3.4 %collective-permute-start.6 = (f32[24,128]{1,0:T(8,128)S(1)}, f32[24,128]{1,0:T(8,128)S(1)}, u32[]{:S(2)}, u32[]{:S(2)}) collective-permute-start(f32[24,128]{1,0:T(8,128)S(1)} %pad_maximum_fusion), channel_id=1, source_target_pairs={{0,3},{1,2},{2,1},{3,0},{4,7},{5,6},{6,5},{7,4},{8,11},{9,10},{10,... | collective-permute-start | bytes 36872 | tf_op jit(solution)/shard_map/ppermute | solution.py:418
  49.7 3.7 %collective-permute-start.7 = (f32[24,128]{1,0:T(8,128)S(1)}, f32[24,128]{1,0:T(8,128)S(1)}, u32[]{:S(2)}, u32[]{:S(2)}) collective-permute-start(f32[24,128]{1,0:T(8,128)S(1)} %pad_maximum_fusion.2), channel_id=1, source_target_pairs={{0,4},{1,5},{2,6},{3,7},{4,0},{5,1},{6,2},{7,3},{8,12},{9,13},{10,... | collective-permute-start | bytes 36872 | tf_op jit(solution)/shard_map/ppermute | solution.py:418
  53.5 4.5 %collective-permute-start.8 = (f32[16,128]{1,0:T(8,128)S(1)}, f32[16,128]{1,0:T(8,128)S(1)}, u32[]{:S(2)}, u32[]{:S(2)}) collective-permute-start(f32[16,128]{1,0:T(8,128)S(1)} %slice_add_fusion), channel_id=1, source_target_pairs={{0,16},{8,24},{16,0},{24,8},{1,17},{9,25},{17,1},{25,9},{2,18},{10... | collective-permute-start | bytes 24584 | tf_op jit(solution)/shard_map/ppermute | solution.py:418

commit v3 on v2

--- a/solution.py
+++ b/solution.py
@@ -314,6 +314,7 @@
 def pair_sums(groups, given, bins, arrays, place, carried, per_cell, last):
     length = arrays[0].shape[1]
     n_arrays, n_carried = len(arrays), len(carried)
+    buffers = 4 if len(groups) < 8 else 2
     span = 2 * NKB
     strip = per_cell * per_cell // length
 
@@ -357,14 +358,14 @@
         sums, others_sums = zeros(), zeros()
         position = turn = 0
         for center, pair in groups:
-            e = chosen.at[turn % 2]
+            e = chosen.at[turn % buffers]
             turn += 1
             for o in range(len(pair)):
                 choose(e, bins[position + o], 0, o * per_cell)
             position += len(pair)
             add(sums, e, center, [edge[1] if center != edge[1] else edge[2] for edge in pair])
         for array, start, a, b in given:
-            e = chosen.at[turn % 2]
+            e = chosen.at[turn % buffers]
             turn += 1
             for i in range(per_cell // strip):
                 piece = arrays[array][start : start + strip, i * per_cell : (i + 1) * per_cell]
@@ -395,7 +396,7 @@
         out_shape=[jax.ShapeDtypeStruct(shape, jnp.float32) for shape in shapes],
         in_specs=vmem(n_arrays + 1 + n_carried),
         out_specs=vmem(len(shapes)),
-        scratch_shapes=[pltpu.VMEM((2, NSEP * per_cell, 2 * per_cell), jnp.bfloat16)],
+        scratch_shapes=[pltpu.VMEM((buffers, NSEP * per_cell, 2 * per_cell), jnp.bfloat16)],
         compiler_params=params(),
         cost_estimate=cost(2 * NSEP * per_cell * per_cell * length * n_edges, 2**20),
     )(*arrays, bins, *carried)

time: 58.9 us -> 58.6 us (level)
  transfers between devices with their start and end apart: 9 -> 9, of which waited for: 7 -> 7; matrix products, arithmetic and copies ran while one was open for 1% -> 1% of each run, Pallas kernels for 19% -> 18%
where the time goes in v3:
time: 58.6 us; the launch traced here: 58.2 us
  waiting for transfers between devices  20.8 us (35%)
  Pallas kernels  19.5 us (33%)
  starting transfers between devices  14.5 us (25%)
  other arithmetic  1.93 us (3%)
  between operations  1.53 us (3%)
    ppermute x4, waiting for transfers between devices, shifted(): lax.ppermute(value, axis, [(i + steps, i) for i in range(count) if 0 <= i...  13.6 us
    pallas_call x3, Pallas kernels, pair_sums(): pl.pallas_call(kernel, out_shape=[jax.ShapeDtypeStruct(shape, jnp.float32...  13.2 us
    ppermute x5, starting transfers between devices, over_mesh(): other = lax.ppermute(message, axis, [(i, i ^ mask) for i in range(count)])  9.18 us
    ppermute x5, waiting for transfers between devices, over_mesh(): other = lax.ppermute(message, axis, [(i, i ^ mask) for i in range(count)])  7.11 us
    ppermute x4, starting transfers between devices, shifted(): lax.ppermute(value, axis, [(i + steps, i) for i in range(count) if 0 <= i...  5.35 us
    pallas_call x1, Pallas kernels, other_cells(): pl.pallas_call(kernel, name='other_cells', out_shape=shapes, in_specs=[hb...  4.09 us
    pallas_call x1, Pallas kernels, end_cells(): pl.pallas_call(kernel, name='end_cells', out_shape=jax.ShapeDtypeStruct((...  2.17 us
  transfers between devices with their start and end apart: 9, of which 7 were waited for; matrix products, arithmetic and copies ran while one was open for 1% of the time, Pallas kernels for 18%

profile of v3, /device:TPU:0, one launch (start us, length us, event | category | flops | bytes accessed | tf_op | source)
XLA Modules:
  0.0 58.2 jit_solution(6662121451848709030)
XLA Ops:
  0.6 0.0 copy-start
  1.4 0.7 %pad_add_fusion.refs_5_ = s32[1,4,1,40]{3,2,1,0:T(1,128)S(1)} fusion(s32[1,1,1,40]{3,2,1,0:T(1,128)S(1)} %compare_convert_fusion, s32[1,3,1,40]{3,2,1,0:T(1,128)} %bitcast.7), kind=kLoop, calls=%fused_computation.15 | loop fusion | flops 160 | bytes 1280 | tf_op jit(solution)/shard_map/concatenate | solution.py:441
  2.1 2.2 %end_cells.1.refs_4_.refs_0_ = bf16[256,1024]{1,0:T(8,128)(2,1)S(1)} custom-call(bf16[2,4,128,1024]{3,2,1,0:T(8,128)(2,1)} %refs_0_.1, s32[2,4,2,128]{3,2,1,0:T(2,128)} %refs_1_.1, f32[2,4,128]{2,1,0:T(4,128)} %refs_2_.1, bf16[2,512,512]{2,1,0:T(8,128)(2,1)} %constant.48.clone.basis.refs_3_), custom_call_target="tpu_custom_call" | custom-call | flops 536870912 | bytes 4194304 | tf_op jit(solution)/shard_map/end_cells/pallas_call | solution.py:206
  4.3 0.0 copy-done
  4.3 4.1 %other_cells.1 = (bf16[256,1024]{1,0:T(8,128)(2,1)S(1)}, bf16[512,1024]{1,0:T(8,128)(2,1)S(1)}, bf16[288,1024]{1,0:T(8,128)(2,1)S(1)}, f32[8,8,128]{2,1,0:T(8,12...) custom-call(bf16[2,4,128,1024]{3,2,1,0:T(8,128)(2,1)} %refs_0_.1, ...), custom_call_target="tpu_custom_call" | custom-call | flops 1610612736 | bytes 8388608 | tf_op jit(solution)/shard_map/other_cells/pallas_call | solution.py:289
  8.4 1.3 %collective-permute-start.3 = (bf16[288,1024]{1,0:T(8,128)(2,1)S(1)}, bf16[288,1024]{1,0:T(8,128)(2,1)S(1)}, u32[]{:S(2)}, u32[]{:S(2)}) collective-permute-start(bf16[288,1024]{1,0:T(8,128)(2,1)S(1)} %get-tuple-element.21), channel_id=1, source_target_pairs={{1,0},{2,1},{3,2},{4,3},{5,4},{6,5},{7,6},{9,8},{10,9},{11,10},{12... | collective-permute-start | bytes 1769480 | tf_op jit(solution)/shard_map/ppermute | solution.py:429
  9.7 1.3 %collective-permute-start = (bf16[256,1024]{1,0:T(8,128)(2,1)S(1)}, bf16[256,1024]{1,0:T(8,128)(2,1)S(1)}, u32[]{:S(2)}, u32[]{:S(2)}) collective-permute-start(bf16[256,1024]{1,0:T(8,128)(2,1)S(1)} %end_cells.1.refs_4_.refs_0_), channel_id=1, source_target_pairs={{8,0},{16,8},{24,16},{9,1},{17,9},{25,17},{10,2},{18,10},{26,18},{... | collective-permute-start | bytes 1572872 | tf_op jit(solution)/shard_map/ppermute | solution.py:429
  11.0 1.3 %collective-permute-start.1 = (bf16[256,1024]{1,0:T(8,128)(2,1)S(1)}, bf16[256,1024]{1,0:T(8,128)(2,1)S(1)}, u32[]{:S(2)}, u32[]{:S(2)}) collective-permute-start(bf16[256,1024]{1,0:T(8,128)(2,1)S(1)} %get-tuple-element.16.refs_1_), channel_id=1, source_target_pairs={{8,0},{16,8},{24,16},{9,1},{17,9},{25,17},{10,2},{18,10},{26,18},{... | collective-permute-start | bytes 1572872 | tf_op jit(solution)/shard_map/ppermute | solution.py:429
  12.3 6.9 %shard_map.86.refs_5_ = f32[2,8,8,128]{3,2,1,0:T(8,128)S(1)} custom-call(bf16[256,1024]{1,0:T(8,128)(2,1)S(1)} %end_cells.1.refs_4_.refs_0_, bf16[256,1024]{1,0:T(8,128)(2,1)S(1)} %get-tuple-element.16.refs_1_, bf16[512,1024]{1,0:T(8,128)(2,1)S(1)} %get-tuple-element.15.refs_2_.refs_1_.refs_0_, bf16[22,128,128]{2,1,0:T(8,128)(2,1)S(1)} %get-tuple-element.17.refs_3_), custom_call_target="tpu_custom_call" | custom-call | flops 5905580032 | bytes 1048576 | tf_op jit(solution)/shard_map/pallas_call | solution.py:394
  19.3 7.7 %collective-permute-done.refs_3_.refs_1_ = bf16[256,1024]{1,0:T(8,128)(2,1)S(1)} collective-permute-done((bf16[256,1024]{1,0:T(8,128)(2,1)S(1)}, bf16[256,1024]{1,0:T(8,128)(2,1)S(1)}, u32[]{:S(2)}, u32[]{:S(2)}) %collective-permute-start) | collective-permute-done | bytes 524320 | tf_op jit(solution)/shard_map/ppermute | solution.py:429
  27.0 1.5 %collective-permute-start.2 = (bf16[128,1024]{1,0:T(8,128)(2,1)S(1)}, bf16[128,1024]{1,0:T(8,128)(2,1)S(1)}, u32[]{:S(2)}, u32[]{:S(2)}) collective-permute-start(bf16[128,1024]{1,0:T(8,128)(2,1)S(1)} %slice.28), channel_id=1, source_target_pairs={{1,0},{2,1},{3,2},{4,3},{5,4},{6,5},{7,6},{9,8},{10,9},{11,10},{12... | collective-permute-start | bytes 786440 | tf_op jit(solution)/shard_map/ppermute | solution.py:429
  28.5 0.0 collective-permute-done.3.refs_2_
  28.5 3.8 %shard_map.87 = (f32[2,8,8,128]{3,2,1,0:T(8,128)S(1)}, f32[8,128]{1,0:T(8,128)S(1)}) custom-call(bf16[256,1024]{1,0:T(8,128)(2,1)S(1)} %end_cells.1.refs_4_.refs_0_, bf16[512,1024]{1,0:T(8,128)(2,1)S(1)} %get-tuple-element.15.refs_2_.refs_1_.refs_0_, bf16[288,1024]{1,0:T(8,128)(2,1)S(1)} %collective-permute-done.3.refs_2_, ...), custom_call_target="tpu_custom_call" | custom-call | flops 2684354560 | bytes 1048576 | tf_op jit(solution)/shard_map/pallas_call | solution.py:394
  32.3 5.9 %collective-permute-done.1.refs_2_ = bf16[256,1024]{1,0:T(8,128)(2,1)S(1)} collective-permute-done((bf16[256,1024]{1,0:T(8,128)(2,1)S(1)}, bf16[256,1024]{1,0:T(8,128)(2,1)S(1)}, u32[]{:S(2)}, u32[]{:S(2)}) %collective-permute-start.1) | collective-permute-done | bytes 524320 | tf_op jit(solution)/shard_map/ppermute | solution.py:429
  38.2 0.0 collective-permute-done.2.refs_3_
  38.2 2.5 %shard_map.88 = (f32[8,128]{1,0:T(8,128)S(1)}, f32[16,128]{1,0:T(8,128)S(1)}) custom-call(bf16[512,1024]{1,0:T(8,128)(2,1)S(1)} %get-tuple-element.15.refs_2_.refs_1_.refs_0_, bf16[256,1024]{1,0:T(8,128)(2,1)S(1)} %collective-permute-done.refs_3_.refs_1_, bf16[256,1024]{1,0:T(8,128)(2,1)S(1)} %collective-permute-done.1.refs_2_, ...), custom_call_target="tpu_custom_call" | custom-call | flops 2147483648 | bytes 1048576 | tf_op jit(solution)/shard_map/pallas_call | solution.py:394
  40.7 2.4 %collective-permute-start.4 = (f32[16,128]{1,0:T(8,128)S(1)}, f32[16,128]{1,0:T(8,128)S(1)}, u32[]{:S(2)}, u32[]{:S(2)}) collective-permute-start(f32[16,128]{1,0:T(8,128)S(1)} %get-tuple-element.27), channel_id=1, source_target_pairs={{0,8},{8,0},{16,24},{24,16},{1,9},{9,1},{17,25},{25,17},{2,10},{10... | collective-permute-start | bytes 24584 | tf_op jit(solution)/shard_map/ppermute | solution.py:419
  43.1 1.6 %collective-permute-done.4 = f32[16,128]{1,0:T(8,128)S(1)} collective-permute-done((f32[16,128]{1,0:T(8,128)S(1)}, f32[16,128]{1,0:T(8,128)S(1)}, u32[]{:S(2)}, u32[]{:S(2)}) %collective-permute-start.4) | collective-permute-done | bytes 8224 | tf_op jit(solution)/shard_map/ppermute | solution.py:419
  44.7 0.0 collective-permute-start.5
  44.7 1.2 %collective-permute-done.5 = f32[24,128]{1,0:T(8,128)S(1)} collective-permute-done((f32[24,128]{1,0:T(8,128)S(1)}, f32[24,128]{1,0:T(8,128)S(1)}, u32[]{:S(2)}, u32[]{:S(2)}) %collective-permute-start.5) | collective-permute-done | bytes 12320 | tf_op jit(solution)/shard_map/ppermute | solution.py:419
  45.9 2.0 %collective-permute-start.6 = (f32[24,128]{1,0:T(8,128)S(1)}, f32[24,128]{1,0:T(8,128)S(1)}, u32[]{:S(2)}, u32[]{:S(2)}) collective-permute-start(f32[24,128]{1,0:T(8,128)S(1)} %pad_maximum_fusion), channel_id=1, source_target_pairs={{0,3},{1,2},{2,1},{3,0},{4,7},{5,6},{6,5},{7,4},{8,11},{9,10},{10,... | collective-permute-start | bytes 36872 | tf_op jit(solution)/shard_map/ppermute | solution.py:419
  47.9 1.4 %collective-permute-done.6 = f32[24,128]{1,0:T(8,128)S(1)} collective-permute-done((f32[24,128]{1,0:T(8,128)S(1)}, f32[24,128]{1,0:T(8,128)S(1)}, u32[]{:S(2)}, u32[]{:S(2)}) %collective-permute-start.6) | collective-permute-done | bytes 12320 | tf_op jit(solution)/shard_map/ppermute | solution.py:419
  49.3 2.0 %collective-permute-start.7 = (f32[24,128]{1,0:T(8,128)S(1)}, f32[24,128]{1,0:T(8,128)S(1)}, u32[]{:S(2)}, u32[]{:S(2)}) collective-permute-start(f32[24,128]{1,0:T(8,128)S(1)} %pad_maximum_fusion.2), channel_id=1, source_target_pairs={{0,4},{1,5},{2,6},{3,7},{4,0},{5,1},{6,2},{7,3},{8,12},{9,13},{10,... | collective-permute-start | bytes 36872 | tf_op jit(solution)/shard_map/ppermute | solution.py:419
  51.4 1.7 %collective-permute-done.7 = f32[24,128]{1,0:T(8,128)S(1)} collective-permute-done((f32[24,128]{1,0:T(8,128)S(1)}, f32[24,128]{1,0:T(8,128)S(1)}, u32[]{:S(2)}, u32[]{:S(2)}) %collective-permute-start.7) | collective-permute-done | bytes 12320 | tf_op jit(solution)/shard_map/ppermute | solution.py:419
  53.1 2.7 %collective-permute-start.8 = (f32[16,128]{1,0:T(8,128)S(1)}, f32[16,128]{1,0:T(8,128)S(1)}, u32[]{:S(2)}, u32[]{:S(2)}) collective-permute-start(f32[16,128]{1,0:T(8,128)S(1)} %slice_add_fusion), channel_id=1, source_target_pairs={{0,16},{8,24},{16,0},{24,8},{1,17},{9,25},{17,1},{25,9},{2,18},{10... | collective-permute-start | bytes 24584 | tf_op jit(solution)/shard_map/ppermute | solution.py:419
  55.8 0.6 %fusion.6 = f32[1,1,8,128]{3,2,1,0:T(8,128)} fusion(f32[8,128]{1,0:T(8,128)S(1)} %get-tuple-element.26, f32[8,128]{1,0:T(8,128)S(1)} %get-tuple-element.25.refs_8_, f32[24,128]{1,0:T(8,128)S(1)} %collective-permute-done.5, f32[24,128]{1,0:T(8,128)S(1)} %collective-permute-done.7, pred[]{:T(512)S(6)} %eq.19, pred[]{:T(512)S(6)} %eq.18, pred[]{:T(512)S(6)} %eq.17, ...), kind=kLoop, calls=%fused_computation.14 | loop fusion | flops 6144 | bytes 24580 | tf_op jit(solution)/shard_map/reshape | solution.py:492
  56.4 1.2 %collective-permute-done.8 = f32[16,128]{1,0:T(8,128)S(1)} collective-permute-done((f32[16,128]{1,0:T(8,128)S(1)}, f32[16,128]{1,0:T(8,128)S(1)}, u32[]{:S(2)}, u32[]{:S(2)}) %collective-permute-start.8) | collective-permute-done | bytes 8224 | tf_op jit(solution)/shard_map/ppermute | solution.py:419
  57.6 0.6 %fusion = f32[8,128]{1,0:T(8,128)} fusion(f32[16,128]{1,0:T(8,128)S(1)} %add.36), kind=kLoop, calls=%fused_computation.7 | loop fusion | flops 2048 | bytes 12288 | tf_op jit(solution)/shard_map/div | solution.py:493
  (11 shorter events, 0.1 us)
Async XLA Ops:
  0.6 3.7 %copy-start = (s32[1,1,40,128,128]{4,3,2,1,0:T(8,128)S(1)}, s32[1,1,40,128,128]{4,3,2,1,0:T(8,128)}, u32[]{:S(2)}) copy-start(s32[1,1,40,128,128]{4,3,2,1,0:T(8,128)} %param.12) | copy-start | bytes 7864324
  8.4 20.1 %collective-permute-start.3 = (bf16[288,1024]{1,0:T(8,128)(2,1)S(1)}, bf16[288,1024]{1,0:T(8,128)(2,1)S(1)}, u32[]{:S(2)}, u32[]{:S(2)}) collective-permute-start(bf16[288,1024]{1,0:T(8,128)(2,1)S(1)} %get-tuple-element.21), channel_id=1, source_target_pairs={{1,0},{2,1},{3,2},{4,3},{5,4},{6,5},{7,6},{9,8},{10,9},{11,10},{12... | collective-permute-start | bytes 1769480 | tf_op jit(solution)/shard_map/ppermute | solution.py:429
  9.7 17.3 %collective-permute-start = (bf16[256,1024]{1,0:T(8,128)(2,1)S(1)}, bf16[256,1024]{1,0:T(8,128)(2,1)S(1)}, u32[]{:S(2)}, u32[]{:S(2)}) collective-permute-start(bf16[256,1024]{1,0:T(8,128)(2,1)S(1)} %end_cells.1.refs_4_.refs_0_), channel_id=1, source_target_pairs={{8,0},{16,8},{24,16},{9,1},{17,9},{25,17},{10,2},{18,10},{26,18},{... | collective-permute-start | bytes 1572872 | tf_op jit(solution)/shard_map/ppermute | solution.py:429
  11.0 27.2 %collective-permute-start.1 = (bf16[256,1024]{1,0:T(8,128)(2,1)S(1)}, bf16[256,1024]{1,0:T(8,128)(2,1)S(1)}, u32[]{:S(2)}, u32[]{:S(2)}) collective-permute-start(bf16[256,1024]{1,0:T(8,128)(2,1)S(1)} %get-tuple-element.16.refs_1_), channel_id=1, source_target_pairs={{8,0},{16,8},{24,16},{9,1},{17,9},{25,17},{10,2},{18,10},{26,18},{... | collective-permute-start | bytes 1572872 | tf_op jit(solution)/shard_map/ppermute | solution.py:429
  27.0 11.2 %collective-permute-start.2 = (bf16[128,1024]{1,0:T(8,128)(2,1)S(1)}, bf16[128,1024]{1,0:T(8,128)(2,1)S(1)}, u32[]{:S(2)}, u32[]{:S(2)}) collective-permute-start(bf16[128,1024]{1,0:T(8,128)(2,1)S(1)} %slice.28), channel_id=1, source_target_pairs={{1,0},{2,1},{3,2},{4,3},{5,4},{6,5},{7,6},{9,8},{10,9},{11,10},{12... | collective-permute-start | bytes 786440 | tf_op jit(solution)/shard_map/ppermute | solution.py:429
  40.7 4.0 %collective-permute-start.4 = (f32[16,128]{1,0:T(8,128)S(1)}, f32[16,128]{1,0:T(8,128)S(1)}, u32[]{:S(2)}, u32[]{:S(2)}) collective-permute-start(f32[16,128]{1,0:T(8,128)S(1)} %get-tuple-element.27), channel_id=1, source_target_pairs={{0,8},{8,0},{16,24},{24,16},{1,9},{9,1},{17,25},{25,17},{2,10},{10... | collective-permute-start | bytes 24584 | tf_op jit(solution)/shard_map/ppermute | solution.py:419
  44.7 1.2 %collective-permute-start.5 = (f32[24,128]{1,0:T(8,128)S(1)}, f32[24,128]{1,0:T(8,128)S(1)}, u32[]{:S(2)}, u32[]{:S(2)}) collective-permute-start(f32[24,128]{1,0:T(8,128)S(1)} %pad_maximum_fusion.1), channel_id=1, source_target_pairs={{0,1},{1,0},{2,3},{3,2},{4,5},{5,4},{6,7},{7,6},{8,9},{9,8},{10,11... | collective-permute-start | bytes 36872 | tf_op jit(solution)/shard_map/ppermute | solution.py:419
  45.9 3.4 %collective-permute-start.6 = (f32[24,128]{1,0:T(8,128)S(1)}, f32[24,128]{1,0:T(8,128)S(1)}, u32[]{:S(2)}, u32[]{:S(2)}) collective-permute-start(f32[24,128]{1,0:T(8,128)S(1)} %pad_maximum_fusion), channel_id=1, source_target_pairs={{0,3},{1,2},{2,1},{3,0},{4,7},{5,6},{6,5},{7,4},{8,11},{9,10},{10,... | collective-permute-start | bytes 36872 | tf_op jit(solution)/shard_map/ppermute | solution.py:419
  49.3 3.7 %collective-permute-start.7 = (f32[24,128]{1,0:T(8,128)S(1)}, f32[24,128]{1,0:T(8,128)S(1)}, u32[]{:S(2)}, u32[]{:S(2)}) collective-permute-start(f32[24,128]{1,0:T(8,128)S(1)} %pad_maximum_fusion.2), channel_id=1, source_target_pairs={{0,4},{1,5},{2,6},{3,7},{4,0},{5,1},{6,2},{7,3},{8,12},{9,13},{10,... | collective-permute-start | bytes 36872 | tf_op jit(solution)/shard_map/ppermute | solution.py:419
  53.1 4.5 %collective-permute-start.8 = (f32[16,128]{1,0:T(8,128)S(1)}, f32[16,128]{1,0:T(8,128)S(1)}, u32[]{:S(2)}, u32[]{:S(2)}) collective-permute-start(f32[16,128]{1,0:T(8,128)S(1)} %slice_add_fusion), channel_id=1, source_target_pairs={{0,16},{8,24},{16,0},{24,8},{1,17},{9,25},{17,1},{25,9},{2,18},{10... | collective-permute-start | bytes 24584 | tf_op jit(solution)/shard_map/ppermute | solution.py:419
